TPU v7x, 32 devices: a whole 2x2x4 slice. The times are simulated.
32 devices in a mesh: seq: 4 (over y, x), fsdp: 8 (over z, core).
Axes of the slice: x: 2, y: 2, z: 4, core: 2. Of those that a mesh axis runs over, the one named last changes fastest.
Arguments:
- inputs: bfloat16 [8, 1536, 768], P(None, ('seq', 'fsdp')), may hold values from -6 to 6
- w_query: bfloat16 [768, 768], P('fsdp'), may hold values from -0.21875 to 0.21875
- w_key: bfloat16 [768, 768], P('fsdp'), may hold values from -0.21875 to 0.21875
- w_value: bfloat16 [768, 768], P('fsdp'), may hold values from -0.21875 to 0.21875
- b_value: bfloat16 [768], P('fsdp'), may hold values from -3 to 3
- w_out: bfloat16 [768, 768], P('fsdp'), may hold values from -0.625 to 0.625
- b_out: bfloat16 [768], P('fsdp'), may hold values from -3 to 3
- norm1_gain: bfloat16 [768], P('fsdp'), may hold values from 0.099609375 to 1.8984375
- norm1_bias: bfloat16 [768], P('fsdp'), may hold values from -3 to 3
- w_in: bfloat16 [768, 3072], P('fsdp'), may hold values from -0.21875 to 0.21875
- b_in: bfloat16 [3072], P('fsdp'), may hold values from -3 to 3
- w_back: bfloat16 [3072, 768], P('fsdp'), may hold values from -0.15625 to 0.15625
- b_back: bfloat16 [768], P('fsdp'), may hold values from -3 to 3
- norm2_gain: bfloat16 [768], P('fsdp'), may hold values from 0.099609375 to 1.8984375
- norm2_bias: bfloat16 [768], P('fsdp'), may hold values from -3 to 3
- w_relative: bfloat16 [768, 12, 64], P('fsdp', 'seq'), may hold values from -0.21875 to 0.21875
- bias_content: bfloat16 [12, 64], P('seq', 'fsdp'), may hold values from -5 to 5
- bias_position: bfloat16 [12, 64], P('seq', 'fsdp'), may hold values from -5 to 5
- bias_type: bfloat16 [12, 64], P('seq', 'fsdp'), may hold values from -5 to 5
- type_embed: bfloat16 [2, 12, 64], P(None, 'seq', 'fsdp'), may hold values from -5 to 5
- lengths: int32 [8, 3], replicated, may hold values from 1 to 1024, 1536 in all within a row
- token_types: int32 [8, 1536], replicated, may hold values from 0 to 1
- owners: int32 [8], replicated, may hold values from 0 to 7, each once
- grad_output: bfloat16 [8, 1536, 768], P('fsdp', 'seq'), may hold values from -6 to 6
Outputs:
- activations: bfloat16 [8, 1536, 768], P('fsdp', 'seq')
- input_grad: bfloat16 [8, 1536, 768], P(None, ('seq', 'fsdp'))
- grad_w_query: float32 [768, 768], P(('seq', 'fsdp'))
- grad_w_key: float32 [768, 768], P(('seq', 'fsdp'))
- grad_w_value: float32 [768, 768], P(('seq', 'fsdp'))
- grad_b_value: float32 [768], P(('seq', 'fsdp'))
- grad_w_out: float32 [768, 768], P(('seq', 'fsdp'))
- grad_b_out: float32 [768], P(('seq', 'fsdp'))
- grad_norm1_gain: float32 [768], P(('seq', 'fsdp'))
- grad_norm1_bias: float32 [768], P(('seq', 'fsdp'))
- grad_w_in: float32 [768, 3072], P(('seq', 'fsdp'))
- grad_b_in: float32 [3072], P(('seq', 'fsdp'))
- grad_w_back: float32 [3072, 768], P(('seq', 'fsdp'))
- grad_b_back: float32 [768], P(('seq', 'fsdp'))
- grad_norm2_gain: float32 [768], P(('seq', 'fsdp'))
- grad_norm2_bias: float32 [768], P(('seq', 'fsdp'))
- grad_w_relative: float32 [768, 12, 64], P('fsdp', 'seq')
- grad_bias_content: float32 [12, 64], P('seq', 'fsdp')
- grad_bias_position: float32 [12, 64], P('seq', 'fsdp')
- grad_bias_type: float32 [12, 64], P('seq', 'fsdp')
- grad_type_embed: float32 [2, 12, 64], P(None, 'seq', 'fsdp')
Inputs may be any that keep to these rules, and one draw needn't show every extreme that they name: Each row holds the lengths of the 3 sequences of one pack, in order; a row sums to 1536 and its largest entry is 1024. Pack j is processed by fsdp index owners[j]; every index owns one pack.
All inputs are finite; a program needn't handle non-finite values.
Results may differ from a plain program's by a relative error of at most 0.017.
The roundings to bfloat16 on the way count: a program that leaves them out, or rounds other values in their place, can miss the bound.
Values may be sent and summed in bfloat16 or wider, within the bound.
No kernel may reach another device: no remote copies, remote signals or barrier semaphores. Data moves between devices by JAX's collectives and lax.ppermute only.
A program may use at most 192 MiB of HBM per device.

v0:
```python
import jax
import jax.numpy as jnp
from jax import lax
from jax.sharding import PartitionSpec as P

HEADS = 12
DH = 64


EPS = 1e-09
NEG = -1e30
HIGH = lax.Precision.HIGHEST


def norm_rows(values, gain_vec, shift_vec):
    center = values - jnp.mean(values, axis=-1, keepdims=True)
    inverse = lax.rsqrt(jnp.mean(center * center, axis=-1, keepdims=True) + EPS)
    normed = center * inverse
    return (normed * gain_vec + shift_vec, normed, inverse)


def norm_back(gradient, normed, inverse, gain_vec):
    scaled = gradient * gain_vec
    inner_term = scaled - jnp.mean(scaled, axis=-1, keepdims=True)
    inner_term = inner_term - normed * jnp.mean(scaled * normed, axis=-1, keepdims=True)
    return (inner_term * inverse, jnp.sum(gradient * normed, axis=0), jnp.sum(gradient, axis=0))


def pack_layout(seq_sizes, row_total):
    seq_ends = jnp.cumsum(seq_sizes)
    row_index = jnp.arange(row_total, dtype=jnp.int32)
    passed = (row_index[:, None] >= seq_ends[None, :]).astype(jnp.int32)
    segment = jnp.sum(passed, axis=1)
    start_row = jnp.sum(passed * seq_sizes[None, :], axis=1)
    return (segment, row_index - start_row)


def angles_of(position, width):
    half_width = width // 2
    rate_table = 10000.0 ** (-(jnp.arange(half_width, dtype=jnp.float32) / half_width))
    turned = position.astype(jnp.float32)[:, None] * rate_table[None, :]
    return (jnp.sin(turned), jnp.cos(turned))


def contract_rows(left, right):
    return lax.dot_general(
        left, right, (((0,), (0,)), ((), ())), preferred_element_type=jnp.float32
    )


def contract_cols(left, right):
    return lax.dot_general(
        left, right, (((1,), (1,)), ((), ())), preferred_element_type=jnp.float32
    )


def shards(
    inputs,
    w_query,
    w_key,
    w_value,
    b_value,
    w_out,
    b_out,
    norm1_gain,
    norm1_bias,
    w_in,
    b_in,
    w_back,
    b_back,
    norm2_gain,
    norm2_bias,
    w_relative,
    bias_content,
    bias_position,
    bias_type,
    type_embed,
    lengths,
    token_types,
    owners,
    grad_output,
):
    fsdp_rank = lax.axis_index("fsdp")
    pack_count = owners.shape[0]
    sliver_rows = inputs.shape[1]
    width = inputs.shape[2]
    half_width = width // 2
    scale = DH ** (-0.5)
    owner_table = owners[None, :] == jnp.arange(pack_count, dtype=jnp.int32)[:, None]
    owner_low = owner_table.astype(jnp.bfloat16)
    dealt = jnp.dot(
        owner_low,
        inputs.reshape(pack_count, sliver_rows * width),
        preferred_element_type=jnp.float32,
    )
    dealt = dealt.astype(jnp.bfloat16).reshape(pack_count, sliver_rows, width)
    mine = lax.all_to_all(dealt, "fsdp", split_axis=0, concat_axis=1, tiled=True)[0]
    row_count = mine.shape[0]
    chosen = (owners == fsdp_rank).astype(jnp.int32)
    pack_types = jnp.sum(chosen[:, None] * token_types, axis=0)
    pack_sizes = jnp.sum(chosen[:, None] * lengths, axis=0)
    gathered = (
        lax.all_gather(w_query, "fsdp", axis=0, tiled=True),
        lax.all_gather(w_key, "fsdp", axis=0, tiled=True),
        lax.all_gather(w_value, "fsdp", axis=0, tiled=True),
        lax.all_gather(w_out, "fsdp", axis=0, tiled=True),
        lax.all_gather(w_in, "fsdp", axis=0, tiled=True),
        lax.all_gather(w_back, "fsdp", axis=0, tiled=True),
        lax.all_gather(b_value, "fsdp", axis=0, tiled=True),
        lax.all_gather(b_out, "fsdp", axis=0, tiled=True),
        lax.all_gather(b_in, "fsdp", axis=0, tiled=True),
        lax.all_gather(b_back, "fsdp", axis=0, tiled=True),
        lax.all_gather(norm1_gain, "fsdp", axis=0, tiled=True),
        lax.all_gather(norm1_bias, "fsdp", axis=0, tiled=True),
        lax.all_gather(norm2_gain, "fsdp", axis=0, tiled=True),
        lax.all_gather(norm2_bias, "fsdp", axis=0, tiled=True),
        lax.all_gather(w_relative, "fsdp", axis=0, tiled=True),
        lax.all_gather(bias_content, "fsdp", axis=1, tiled=True),
        lax.all_gather(bias_position, "fsdp", axis=1, tiled=True),
        lax.all_gather(bias_type, "fsdp", axis=1, tiled=True),
        lax.all_gather(type_embed, "fsdp", axis=2, tiled=True),
    )
    (
        wq_full,
        wk_full,
        wv_full,
        wo_full,
        win_full,
        wback_full,
        bv_full,
        bo_full,
        bin_full,
        bback_full,
        gain_one,
        shift_one,
        gain_two,
        shift_two,
        wrel_full,
        content_full,
        position_full,
        typebias_full,
        embed_full,
    ) = gathered
    gain_one = gain_one.astype(jnp.float32)
    shift_one = shift_one.astype(jnp.float32)
    gain_two = gain_two.astype(jnp.float32)
    shift_two = shift_two.astype(jnp.float32)
    embed32 = embed_full.astype(jnp.float32)
    query_rows = jnp.dot(mine, wq_full, preferred_element_type=jnp.float32).astype(jnp.bfloat16)
    key_rows = jnp.dot(mine, wk_full, preferred_element_type=jnp.float32).astype(jnp.bfloat16)
    value_rows = (
        jnp.dot(mine, wv_full, preferred_element_type=jnp.float32) + bv_full.astype(jnp.float32)
    ).astype(jnp.bfloat16)
    head_q, head_k, head_v = (
        lax.all_to_all(
            query_rows.reshape(row_count, HEADS, DH), "seq", split_axis=1, concat_axis=0, tiled=True
        ),
        lax.all_to_all(
            key_rows.reshape(row_count, HEADS, DH), "seq", split_axis=1, concat_axis=0, tiled=True
        ),
        lax.all_to_all(
            value_rows.reshape(row_count, HEADS, DH), "seq", split_axis=1, concat_axis=0, tiled=True
        ),
    )
    pack_rows = head_q.shape[0]
    local_heads = head_q.shape[1]
    segment, position = pack_layout(pack_sizes, pack_rows)
    query32 = head_q.astype(jnp.float32)
    content_q = ((query32 + content_full.astype(jnp.float32)) * scale).astype(jnp.bfloat16)
    position_q = ((query32 + position_full.astype(jnp.float32)) * scale).astype(jnp.bfloat16)
    typed_q = (query32 + typebias_full.astype(jnp.float32)) * scale
    type_score = jnp.einsum("nhe,the->nht", typed_q, embed32, precision=HIGH)
    rel_proj = jnp.einsum("nhe,dhe->nhd", position_q, wrel_full, preferred_element_type=jnp.float32)
    sine, cosine = angles_of(position, width)
    first_half = rel_proj[..., :half_width]
    second_half = rel_proj[..., half_width:]
    query_pos = jnp.concatenate(
        [
            first_half * sine[:, None, :] + second_half * cosine[:, None, :],
            second_half * sine[:, None, :] - first_half * cosine[:, None, :],
        ],
        axis=-1,
    ).astype(jnp.bfloat16)
    key_pos = jnp.concatenate([cosine, sine], axis=-1).astype(jnp.bfloat16)
    block_rows = min(512, pack_rows)
    block_count = pack_rows // block_rows

    def blocked(values):
        return values.reshape((block_count, block_rows) + values.shape[1:])

    def scores_of(block_cq, block_pq, block_ts, block_kind, block_part):
        raw_score = jnp.einsum("ihe,jhe->hij", block_cq, head_k, preferred_element_type=jnp.float32)
        raw_score = raw_score + jnp.einsum(
            "ihd,jd->hij", block_pq, key_pos, preferred_element_type=jnp.float32
        )
        same_kind = block_kind[:, None] == pack_types[None, :]
        raw_score = raw_score + jnp.where(
            same_kind[None],
            jnp.transpose(block_ts[..., 1])[:, :, None],
            jnp.transpose(block_ts[..., 0])[:, :, None],
        )
        allowed = block_part[:, None] == segment[None, :]
        return (raw_score, same_kind, allowed)

    def attend(block):
        block_cq, block_pq, block_ts, block_kind, block_part = block
        raw_score, same_kind, allowed = scores_of(
            block_cq, block_pq, block_ts, block_kind, block_part
        )
        masked = jnp.where(allowed[None], raw_score, NEG)
        row_max = jnp.max(masked, axis=-1, keepdims=True)
        exponent = jnp.exp(masked - row_max)
        row_sum = jnp.sum(exponent, axis=-1, keepdims=True)
        probs = exponent / row_sum
        mixed_out = jnp.einsum(
            "hij,jhe->ihe", probs.astype(jnp.bfloat16), head_v, preferred_element_type=jnp.float32
        )
        return (mixed_out.astype(jnp.bfloat16), (row_max + jnp.log(row_sum))[..., 0])

    block_inputs = (
        blocked(content_q),
        blocked(query_pos),
        blocked(type_score),
        blocked(pack_types),
        blocked(segment),
    )
    head_out, log_sums = lax.map(attend, block_inputs)
    head_out = head_out.reshape(pack_rows, local_heads, DH)
    mixed_rows = lax.all_to_all(head_out, "seq", split_axis=0, concat_axis=1, tiled=True)
    attn_rows = mixed_rows.reshape(row_count, width)
    branch = jnp.dot(attn_rows, wo_full, preferred_element_type=jnp.float32) + bo_full.astype(
        jnp.float32
    )
    first_sum = mine.astype(jnp.float32) + branch
    hidden_one, normed_one, inverse_one = norm_rows(first_sum, gain_one, shift_one)
    hidden_low = hidden_one.astype(jnp.bfloat16)
    pre_act = jnp.dot(hidden_low, win_full, preferred_element_type=jnp.float32) + bin_full.astype(
        jnp.float32
    )
    act_low = jax.nn.gelu(pre_act).astype(jnp.bfloat16)
    ffn_out = jnp.dot(act_low, wback_full, preferred_element_type=jnp.float32) + bback_full.astype(
        jnp.float32
    )
    second_sum = hidden_one + ffn_out
    result, normed_two, inverse_two = norm_rows(second_sum, gain_two, shift_two)
    activations = result.astype(jnp.bfloat16).reshape(1, row_count, width)
    wq_back, wk_back, wv_back, wo_back = (wq_full, wk_full, wv_full, wo_full)
    win_back, wback_back, wrel_back = (win_full, wback_full, wrel_full)
    out_grad = grad_output[0].astype(jnp.float32)
    sum_two_grad, gain_two_grad, shift_two_grad = norm_back(
        out_grad, normed_two, inverse_two, gain_two
    )
    ffn_grad = sum_two_grad.astype(jnp.bfloat16)
    back_bias_grad = jnp.sum(ffn_grad.astype(jnp.float32), axis=0)
    w_back_grad = contract_rows(act_low, ffn_grad)
    act_grad = contract_cols(ffn_grad, wback_back)
    pre_grad = jax.vjp(jax.nn.gelu, pre_act)[1](act_grad)[0].astype(jnp.bfloat16)
    in_bias_grad = jnp.sum(pre_grad.astype(jnp.float32), axis=0)
    w_in_grad = contract_rows(hidden_low, pre_grad)
    hidden_grad = sum_two_grad + contract_cols(pre_grad, win_back)
    sum_one_grad, gain_one_grad, shift_one_grad = norm_back(
        hidden_grad, normed_one, inverse_one, gain_one
    )
    branch_grad = sum_one_grad.astype(jnp.bfloat16)
    out_bias_grad = jnp.sum(branch_grad.astype(jnp.float32), axis=0)
    w_out_grad = contract_rows(attn_rows, branch_grad)
    attn_grad = (
        contract_cols(branch_grad, wo_back).astype(jnp.bfloat16).reshape(row_count, HEADS, DH)
    )
    head_grad = lax.all_to_all(attn_grad, "seq", split_axis=1, concat_axis=0, tiled=True)

    def attend_back(carry, block):
        key_grad, value_grad = carry
        block_cq, block_pq, block_ts, block_kind, block_part, block_lse, block_dout = block
        raw_score, same_kind, allowed = scores_of(
            block_cq, block_pq, block_ts, block_kind, block_part
        )
        probs = jnp.where(allowed[None], jnp.exp(raw_score - block_lse[:, :, None]), 0.0)
        prob_grad = jnp.einsum(
            "ihe,jhe->hij", block_dout, head_v, preferred_element_type=jnp.float32
        )
        row_dot = jnp.sum(probs * prob_grad, axis=-1, keepdims=True)
        score_grad = (probs * (prob_grad - row_dot)).astype(jnp.bfloat16)
        value_grad = value_grad + jnp.einsum(
            "hij,ihe->jhe",
            probs.astype(jnp.bfloat16),
            block_dout,
            preferred_element_type=jnp.float32,
        )
        key_grad = key_grad + jnp.einsum(
            "hij,ihe->jhe", score_grad, block_cq, preferred_element_type=jnp.float32
        )
        cq_grad = jnp.einsum("hij,jhe->ihe", score_grad, head_k, preferred_element_type=jnp.float32)
        pq_grad = jnp.einsum("hij,jd->ihd", score_grad, key_pos, preferred_element_type=jnp.float32)
        same_float = same_kind.astype(jnp.float32)[None]
        score32 = score_grad.astype(jnp.float32)
        type_grad = jnp.stack(
            [
                jnp.sum(score32 * (1.0 - same_float), axis=-1),
                jnp.sum(score32 * same_float, axis=-1),
            ],
            axis=-1,
        )
        return ((key_grad, value_grad), (cq_grad, pq_grad, jnp.transpose(type_grad, (1, 0, 2))))

    zero_heads = jnp.zeros((pack_rows, local_heads, DH), jnp.float32)
    back_inputs = block_inputs + (log_sums, blocked(head_grad))
    (key_grad, value_grad), (cq_grad, pq_grad, type_grad) = lax.scan(
        attend_back, (zero_heads, zero_heads), back_inputs
    )
    cq_grad = cq_grad.reshape(pack_rows, local_heads, DH)
    pq_grad = pq_grad.reshape(pack_rows, local_heads, width)
    type_grad = type_grad.reshape(pack_rows, local_heads, 2)
    first_grad = pq_grad[..., :half_width]
    second_grad = pq_grad[..., half_width:]
    proj_grad = jnp.concatenate(
        [
            first_grad * sine[:, None, :] - second_grad * cosine[:, None, :],
            first_grad * cosine[:, None, :] + second_grad * sine[:, None, :],
        ],
        axis=-1,
    ).astype(jnp.bfloat16)
    position_q_grad = jnp.einsum(
        "nhd,dhe->nhe", proj_grad, wrel_back, preferred_element_type=jnp.float32
    )
    relative_grad = jnp.einsum(
        "nhd,nhe->dhe", proj_grad, position_q, preferred_element_type=jnp.float32
    )
    typed_grad = jnp.einsum("nht,the->nhe", type_grad, embed32, precision=HIGH)
    embed_grad = jnp.einsum("nht,nhe->the", type_grad, typed_q, precision=HIGH)
    content_bias_grad = jnp.sum(cq_grad, axis=0) * scale
    position_bias_grad = jnp.sum(position_q_grad, axis=0) * scale
    type_bias_grad = jnp.sum(typed_grad, axis=0) * scale
    query_grad = ((cq_grad + position_q_grad + typed_grad) * scale).astype(jnp.bfloat16)
    back_q, back_k, back_v = (
        lax.all_to_all(query_grad, "seq", split_axis=0, concat_axis=1, tiled=True),
        lax.all_to_all(
            key_grad.astype(jnp.bfloat16), "seq", split_axis=0, concat_axis=1, tiled=True
        ),
        lax.all_to_all(
            value_grad.astype(jnp.bfloat16), "seq", split_axis=0, concat_axis=1, tiled=True
        ),
    )
    q_rows_grad = back_q.reshape(row_count, width)
    k_rows_grad = back_k.reshape(row_count, width)
    v_rows_grad = back_v.reshape(row_count, width)
    value_bias_grad = jnp.sum(v_rows_grad.astype(jnp.float32), axis=0)
    w_query_grad = contract_rows(mine, q_rows_grad)
    w_key_grad = contract_rows(mine, k_rows_grad)
    w_value_grad = contract_rows(mine, v_rows_grad)
    input_rows = (
        sum_one_grad
        + contract_cols(q_rows_grad, wq_back)
        + contract_cols(k_rows_grad, wk_back)
        + contract_cols(v_rows_grad, wv_back)
    ).astype(jnp.bfloat16)
    returned = lax.all_to_all(
        input_rows.reshape(1, row_count, width), "fsdp", split_axis=1, concat_axis=0, tiled=True
    )
    input_grad = contract_rows(owner_low, returned.reshape(pack_count, sliver_rows * width))
    input_grad = input_grad.astype(jnp.bfloat16).reshape(pack_count, sliver_rows, width)
    reduced = (
        lax.psum_scatter(w_query_grad, ("seq", "fsdp"), scatter_dimension=0, tiled=True),
        lax.psum_scatter(w_key_grad, ("seq", "fsdp"), scatter_dimension=0, tiled=True),
        lax.psum_scatter(w_value_grad, ("seq", "fsdp"), scatter_dimension=0, tiled=True),
        lax.psum_scatter(w_out_grad, ("seq", "fsdp"), scatter_dimension=0, tiled=True),
        lax.psum_scatter(w_in_grad, ("seq", "fsdp"), scatter_dimension=0, tiled=True),
        lax.psum_scatter(w_back_grad, ("seq", "fsdp"), scatter_dimension=0, tiled=True),
        lax.psum_scatter(value_bias_grad, ("seq", "fsdp"), scatter_dimension=0, tiled=True),
        lax.psum_scatter(out_bias_grad, ("seq", "fsdp"), scatter_dimension=0, tiled=True),
        lax.psum_scatter(in_bias_grad, ("seq", "fsdp"), scatter_dimension=0, tiled=True),
        lax.psum_scatter(back_bias_grad, ("seq", "fsdp"), scatter_dimension=0, tiled=True),
        lax.psum_scatter(gain_one_grad, ("seq", "fsdp"), scatter_dimension=0, tiled=True),
        lax.psum_scatter(shift_one_grad, ("seq", "fsdp"), scatter_dimension=0, tiled=True),
        lax.psum_scatter(gain_two_grad, ("seq", "fsdp"), scatter_dimension=0, tiled=True),
        lax.psum_scatter(shift_two_grad, ("seq", "fsdp"), scatter_dimension=0, tiled=True),
    )
    head_reduced = (
        lax.psum_scatter(relative_grad, "fsdp", scatter_dimension=0, tiled=True),
        lax.psum_scatter(content_bias_grad, "fsdp", scatter_dimension=1, tiled=True),
        lax.psum_scatter(position_bias_grad, "fsdp", scatter_dimension=1, tiled=True),
        lax.psum_scatter(type_bias_grad, "fsdp", scatter_dimension=1, tiled=True),
        lax.psum_scatter(embed_grad, "fsdp", scatter_dimension=2, tiled=True),
    )
    return (
        activations,
        input_grad,
        reduced[0],
        reduced[1],
        reduced[2],
        reduced[6],
        reduced[3],
        reduced[7],
        reduced[10],
        reduced[11],
        reduced[4],
        reduced[8],
        reduced[5],
        reduced[9],
        reduced[12],
        reduced[13],
        head_reduced[0],
        head_reduced[1],
        head_reduced[2],
        head_reduced[3],
        head_reduced[4],
    )


def solution(mesh):
    placed = (
        P(None, ("seq", "fsdp"), None),
        P("fsdp", None),
        P("fsdp", None),
        P("fsdp", None),
        P("fsdp"),
        P("fsdp", None),
        P("fsdp"),
        P("fsdp"),
        P("fsdp"),
        P("fsdp", None),
        P("fsdp"),
        P("fsdp", None),
        P("fsdp"),
        P("fsdp"),
        P("fsdp"),
        P("fsdp", "seq", None),
        P("seq", "fsdp"),
        P("seq", "fsdp"),
        P("seq", "fsdp"),
        P(None, "seq", "fsdp"),
        P(),
        P(),
        P(),
        P("fsdp", "seq", None),
    )
    return jax.shard_map(
        shards,
        mesh=mesh,
        in_specs=placed,
        out_specs=(
            P("fsdp", "seq", None),
            P(None, ("seq", "fsdp"), None),
            P(("seq", "fsdp"), None),
            P(("seq", "fsdp"), None),
            P(("seq", "fsdp"), None),
            P(("seq", "fsdp")),
            P(("seq", "fsdp"), None),
            P(("seq", "fsdp")),
            P(("seq", "fsdp")),
            P(("seq", "fsdp")),
            P(("seq", "fsdp"), None),
            P(("seq", "fsdp")),
            P(("seq", "fsdp"), None),
            P(("seq", "fsdp")),
            P(("seq", "fsdp")),
            P(("seq", "fsdp")),
            P("fsdp", "seq", None),
            P("seq", "fsdp"),
            P("seq", "fsdp"),
            P("seq", "fsdp"),
            P(None, "seq", "fsdp"),
        ),
        check_vma=False,
    )
```

profile of v0, /device:TPU:0, one launch (start us, length us, event | category | flops | bytes accessed | tf_op | source)
XLA Modules:
  0.0 1218.5 jit_solution(3819650948097044411)
XLA Ops:
  13.2 6.4 all-to-all-start
  24.0 39.8 %all-reduce.21 = (bf16[768]{0:T(1024)(128)(2,1)S(1)}, bf16[768]{0:T(1024)(128)(2,1)}, bf16[768]{0:T(1024)(128)(2,1)}, bf16[768]{0:T(1024)(128)(2,1)}, bf16[768]{...) all-reduce(bf16[768]{0:T(1024)(128)(2,1)S(1)} %dynamic-update-slice, ...), channel_id=1, replica_groups=mesh['seq'=4,'fsdp'=8] {'fsdp'}, use_global_device_ids=true, to_apply=%add | all-reduce | flops 5376 | bytes 21504
  64.4 8.4 all-gather
  72.9 10.5 all-gather.1
  83.4 9.2 all-gather.2
  93.2 10.1 fusion.80
  139.8 14.7 %all_gather.63 = bf16[2,3,64]{1,0,2:T(2,128)(2,1)S(1)} all-gather(bf16[2,3,8]{1,0,2:T(2,128)(2,1)S(1)} %copy.254), channel_id=1, replica_groups=mesh['seq'=4,'fsdp'=8] {'fsdp'}, dimensions={2}, use_global_device_ids=true | all-gather | bytes 864 | tf_op jit(solution)/shard_map/all_gather | solution.py:121
  155.5 20.3 %all_gather.61 = bf16[768,3,64]{2,1,0:T(4,128)(2,1)} all-gather(bf16[96,3,64]{2,1,0:T(4,128)(2,1)S(1)} %copy.249), channel_id=1, replica_groups=mesh['seq'=4,'fsdp'=8] {'fsdp'}, dimensions={0}, use_global_device_ids=true | all-gather | bytes 331776 | tf_op jit(solution)/shard_map/all_gather | solution.py:117
  195.0 6.6 pad_maximum_fusion
  201.6 6.5 copy.286
  208.1 46.5 %while.31 = (s32[]{:T(128)}, bf16[3,512,3,64]{1,3,2,0:T(8,128)(2,1)S(1)}, f32[3,3,512]{2,1,0:T(4,128)S(1)}, s32[3,512]{1,0:T(4,128)S(1)}, s32[1536]{0:T(1024)S(1...) while((s32[]{:T(128)}, ...), condition=%wide.region_8.9_spmd, body=%wide.region_5.8_spmd.sunk | while | flops 4253121024 | bytes 56772776 | solution.py:227
  209.6 6.3 fusion.190
  224.9 6.3 fusion.190
  240.3 6.3 fusion.190
  264.9 12.9 %all-gather.3 = bf16[8,1,384]{2,1,0:T(2,128)(2,1)S(1)} all-gather(bf16[1,1,384]{2,1,0:T(2,128)(2,1)S(1)} %reshape.534), channel_id=1, replica_groups=mesh['seq'=4,'fsdp'=8] {'fsdp'}, dimensions={0}, use_global_device_ids=true | all-gather | bytes 6912 | tf_op jit(solution)/shard_map/all_gather | solution.py:111
  285.4 6.6 convolution_add_fusion
  292.0 6.9 fusion.111
  302.2 5.5 convert_reduce_fusion
  318.6 9.2 all-to-all-done.5
  329.8 137.2 %while.32 = (s32[]{:T(128)}, f32[1536,3,64]{0,2,1:T(8,128)}, f32[1536,3,64]{0,2,1:T(8,128)S(1)}, f32[3,512,3,64]{1,3,2,0:T(8,128)}, f32[3,512,3,768]{3,1,0,2:T(8...) while((s32[]{:T(128)}, f32[1536,3,64]{0,2,1:T(8,128)}, ...), condition=%wide.region_21.22_spmd.clone, body=%wide.region_17.21_spmd.clone.sunk | while | flops 8801352704 | bytes 177281488 | solution.py:308
  334.1 8.0 fusion.208
  342.1 9.7 multiply_reduce_fusion.9
  351.7 7.1 fusion.209
  358.9 5.0 fusion.211
  370.2 5.4 bitcast_dynamic-update-slice_fusion.5
  379.8 8.0 fusion.208
  387.8 9.7 multiply_reduce_fusion.9
  397.5 7.1 fusion.209
  415.9 5.4 bitcast_dynamic-update-slice_fusion.5
  425.6 8.0 fusion.208
  433.6 9.7 multiply_reduce_fusion.9
  443.3 7.1 fusion.209
  450.4 5.0 fusion.211
  461.7 5.4 bitcast_dynamic-update-slice_fusion.5
  467.1 7.8 subtract_convert_fusion
  488.2 12.5 %all_to_all.138 = bf16[4,2,36864]{2,1,0:T(2,128)(2,1)S(1)} all-to-all(bf16[4,2,36864]{2,1,0:T(2,128)(2,1)} %reshape.575), channel_id=1, replica_groups=mesh['seq'=4,'fsdp'=8] {'seq'}, dimensions={0} | all-to-all | bytes 1179648 | tf_op jit(solution)/shard_map/all_to_all | solution.py:337
  512.3 10.1 all_to_all.139
  538.5 10.8 all_to_all.140
  558.2 9.4 fusion.93
  568.9 7.0 fusion.103
  586.0 5.2 reduce.5
  596.9 22.5 %all-reduce.20 = (f32[3,64]{1,0:T(4,128)S(1)}, f32[3,64]{1,0:T(4,128)S(1)}, f32[3,64]{1,0:T(4,128)S(1)}, f32[2,3,64]{2,0,1:T(2,128)S(1)}) all-reduce(f32[3,64]{1,0:T(4,128)S(1)} %broadcast_multiply_fusion.2, f32[3,64]{1,0:T(4,128)S(1)} %broadcast_multiply_fusion.1, ...), channel_id=17, replica_groups=mesh['seq'=4,'fsdp'=8] {'fsdp'}, use_global_device_ids=true, to_apply=%region_46.47.clone | all-reduce | flops 960 | bytes 7680
  623.6 40.0 %all-reduce.19 = (f32[768]{0:T(1024)S(1)}, f32[768]{0:T(1024)S(1)}, f32[768]{0:T(1024)S(1)}, f32[768]{0:T(1024)S(1)}, f32[3072]{0:T(1024)S(1)}, /*index=5*/f32[7...) all-reduce(f32[768]{0:T(1024)S(1)} %reduce_sum.258, ...), channel_id=5, replica_groups=mesh['seq'=4,'fsdp'=8] {'seq','fsdp'}, use_global_device_ids=true, to_apply=%region_26.27.clone | all-reduce | flops 8448 | bytes 67584
  675.6 44.1 %reduce-scatter.16.cloned.1.call-done = f32[24,768]{1,0:T(8,128)} async-done(((f32[768,768]{1,0:T(8,128)}), f32[24,768]{1,0:T(8,128)}) %reduce-scatter.16.cloned.1.call-update) | async-done | bytes 73744 | tf_op jit(solution)/shard_map/reduce_scatter | solution.py:364
  719.7 104.4 %reduce-scatter.18.cloned.1.call-done = f32[24,768]{1,0:T(8,128)} async-done(((f32[768,768]{1,0:T(8,128)}), f32[24,768]{1,0:T(8,128)}) %reduce-scatter.18.cloned.1.call-update) | async-done | bytes 73744 | tf_op jit(solution)/shard_map/reduce_scatter | solution.py:365
  824.1 104.5 %reduce-scatter.14.cloned.1.call-done = f32[24,768]{1,0:T(8,128)} async-done(((f32[768,768]{1,0:T(8,128)}), f32[24,768]{1,0:T(8,128)}) %reduce-scatter.14.cloned.1.call-update) | async-done | bytes 73744 | tf_op jit(solution)/shard_map/reduce_scatter | solution.py:363
  928.6 141.5 %reduce-scatter.24.cloned.1.call-done = f32[96,768]{1,0:T(8,128)} async-done(((f32[3072,768]{1,0:T(8,128)}), f32[96,768]{1,0:T(8,128)}) %reduce-scatter.24.cloned.1.call-update) | async-done | bytes 294928 | tf_op jit(solution)/shard_map/reduce_scatter | solution.py:368
  1070.1 141.6 %reduce-scatter.22.cloned.1.call-done = f32[24,3072]{1,0:T(8,128)} async-done(((f32[768,3072]{1,0:T(8,128)}), f32[24,3072]{1,0:T(8,128)}) %reduce-scatter.22.cloned.1.call-update) | async-done | bytes 294928 | tf_op jit(solution)/shard_map/reduce_scatter | solution.py:367
  (480 shorter events, 246.1 us)
Async XLA Ops:
  7.2 96.1 %all-gather.15.cloned.1.call-start = ((), (), s32[]{:S(2)}) async-start(), calls=%async_computation.19 | async-start | bytes 1327104 | tf_op jit(solution)/shard_map/all_gather | solution.py:105
  7.9 103.8 %all-gather.13.cloned.1.call-start = ((), (), s32[]{:S(2)}) async-start(), calls=%async_computation.18 | async-start | bytes 1327104 | tf_op jit(solution)/shard_map/all_gather | solution.py:104
  8.7 115.8 %all-gather.11.cloned.1.call-start = ((), (), s32[]{:S(2)}) async-start(), calls=%async_computation.17 | async-start | bytes 1327104 | tf_op jit(solution)/shard_map/all_gather | solution.py:103
  9.4 273.4 %all-gather.17.cloned.1.call-start = ((), (), s32[]{:S(2)}) async-start(), calls=%async_computation.20 | async-start | bytes 1327104 | tf_op jit(solution)/shard_map/all_gather | solution.py:106
  10.0 275.4 %all-gather.19.cloned.1.call-start = ((), (), s32[]{:S(2)}) async-start(), calls=%async_computation.21 | async-start | bytes 5308416 | tf_op jit(solution)/shard_map/all_gather | solution.py:107
  11.9 10.7 copy-start.80
  11.9 11.0 copy-start.81
  11.9 11.2 copy-start.82
  11.9 11.4 copy-start.83
  11.9 11.6 copy-start.84
  11.9 11.9 copy-start.85
  11.9 52.5 %copy-start.74 = (bf16[3,8]{1,0:T(4,128)(2,1)S(1)}, bf16[3,8]{1,0:T(4,128)(2,1)}, u32[]{:S(2)}) copy-start(bf16[3,8]{1,0:T(4,128)(2,1)} %param.44) | copy-start | bytes 148
  11.9 60.9 %copy-start.75 = (bf16[3,8]{1,0:T(4,128)(2,1)S(1)}, bf16[3,8]{1,0:T(4,128)(2,1)}, u32[]{:S(2)}) copy-start(bf16[3,8]{1,0:T(4,128)(2,1)} %param.45) | copy-start | bytes 148
  12.0 71.4 %copy-start.76 = (bf16[3,8]{1,0:T(4,128)(2,1)S(1)}, bf16[3,8]{1,0:T(4,128)(2,1)}, u32[]{:S(2)}) copy-start(bf16[3,8]{1,0:T(4,128)(2,1)} %param.46) | copy-start | bytes 148
  13.2 90.1 %all-to-all-start = ((bf16[8,48,768]{2,1,0:T(8,128)(2,1)}), bf16[8,48,768]{2,1,0:T(8,128)(2,1)S(1)}, u32[]{:S(2)}, u32[]{:S(2)}) async-start(bf16[8,48,768]{2,1,0:T(8,128)(2,1)} %copy.241), calls=%async_computation | async-start | bytes 1179648 | tf_op jit(solution)/shard_map/all_to_all | solution.py:97
  19.6 272.4 %all-gather.21.cloned.1.call-start = ((), (), s32[]{:S(2)}) async-start(), calls=%async_computation.22 | async-start | bytes 5308416 | tf_op jit(solution)/shard_map/all_gather | solution.py:108
  103.3 21.1 %copy-start.14 = (bf16[8,48,768]{2,1,0:T(8,128)(2,1)}, bf16[8,48,768]{2,1,0:T(8,128)(2,1)S(1)}, u32[]{:S(2)}) copy-start(bf16[8,48,768]{2,1,0:T(8,128)(2,1)S(1)} %all-to-all-done) | copy-start | bytes 1769476
  106.5 13.1 %all-to-all-start.3 = ((bf16[384,12,64]{0,2,1:T(8,128)(2,1)}), bf16[384,12,64]{0,2,1:T(8,128)(2,1)S(1)}, u32[]{:S(2)}, u32[]{:S(2)}) async-start(bf16[384,12,64]{0,2,1:T(8,128)(2,1)} %bitcast.394), calls=%async_computation.3 | async-start | bytes 1179648 | tf_op jit(solution)/shard_map/all_to_all | solution.py:161
  119.7 12.6 %all-to-all-start.2 = ((bf16[384,12,64]{0,2,1:T(8,128)(2,1)}), bf16[384,12,64]{0,2,1:T(8,128)(2,1)}, u32[]{:S(2)}, u32[]{:S(2)}) async-start(bf16[384,12,64]{0,2,1:T(8,128)(2,1)} %bitcast.392), calls=%async_computation.2 | async-start | bytes 1179648 | tf_op jit(solution)/shard_map/all_to_all | solution.py:158
  124.4 11.3 copy-start.64
  124.4 12.2 %copy-start.73 = (bf16[2,3,8]{2,0,1:T(2,128)(2,1)S(1)}, bf16[2,3,8]{2,0,1:T(2,128)(2,1)}, u32[]{:S(2)}) copy-start(bf16[2,3,8]{2,0,1:T(2,128)(2,1)} %param.47) | copy-start | bytes 292
  132.3 48.5 %all-to-all-start.1 = ((bf16[384,12,64]{0,2,1:T(8,128)(2,1)}), bf16[384,12,64]{0,2,1:T(8,128)(2,1)S(1)}, u32[]{:S(2)}, u32[]{:S(2)}) async-start(bf16[384,12,64]{0,2,1:T(8,128)(2,1)} %bitcast.18), calls=%async_computation.1 | async-start | bytes 1179648 | tf_op jit(solution)/shard_map/all_to_all | solution.py:155
  138.9 49.7 %copy-start.46 = (f32[64,3]{0,1:T(4,128)}, f32[64,3]{0,1:T(4,128)S(1)}, u32[]{:S(2)}) copy-start(f32[64,3]{0,1:T(4,128)S(1)} %reshape.552) | copy-start | bytes 2308
  139.7 41.4 %copy-start.50 = (f32[64,3]{0,1:T(4,128)}, f32[64,3]{0,1:T(4,128)S(1)}, u32[]{:S(2)}) copy-start(f32[64,3]{0,1:T(4,128)S(1)} %reshape.553) | copy-start | bytes 2308
  154.5 26.6 %copy-start.55 = (bf16[2,3,64]{2,0,1:T(2,128)(2,1)}, bf16[2,3,64]{2,0,1:T(2,128)(2,1)S(1)}, u32[]{:S(2)}) copy-start(bf16[2,3,64]{2,0,1:T(2,128)(2,1)S(1)} %copy.255) | copy-start | bytes 2308
  177.2 11.5 copy-start.30
  260.8 17.1 %all-to-all-start.4 = ((bf16[4,2,36864]{2,1,0:T(2,128)(2,1)}), bf16[4,2,36864]{2,1,0:T(2,128)(2,1)S(1)}, u32[]{:S(2)}, u32[]{:S(2)}) async-start(bf16[4,2,36864]{2,1,0:T(2,128)(2,1)} %reshape.571), calls=%async_computation.4 | async-start | bytes 1179648 | tf_op jit(solution)/shard_map/all_to_all | solution.py:229
  264.7 18.1 %copy-start.15 = (bf16[8,48,768]{2,1,0:T(8,128)(2,1)S(1)}, bf16[8,48,768]{2,1,0:T(8,128)(2,1)}, u32[]{:S(2)}) copy-start(bf16[8,48,768]{2,1,0:T(8,128)(2,1)} %copy-done.14) | copy-start | bytes 1769476
  264.8 45.8 %copy-start.39 = (f32[768]{0:T(1024)}, f32[768]{0:T(1024)S(1)}, u32[]{:S(2)}) copy-start(f32[768]{0:T(1024)S(1)} %convert_element_type.198) | copy-start | bytes 9220
  264.8 27.2 %copy-start.41 = (f32[768]{0:T(1024)}, f32[768]{0:T(1024)S(1)}, u32[]{:S(2)}) copy-start(f32[768]{0:T(1024)S(1)} %convert_element_type.199) | copy-start | bytes 9220
  285.0 25.6 %copy-start.12 = (f32[384,768]{1,0:T(8,128)}, f32[384,768]{1,0:T(8,128)S(1)}, u32[]{:S(2)}) copy-start(f32[384,768]{1,0:T(8,128)S(1)} %get-tuple-element.740) | copy-start | bytes 3538948
  285.0 25.6 %copy-start.43 = (f32[384]{0:T(512)}, f32[384]{0:T(512)S(1)}, u32[]{:S(2)}) copy-start(f32[384]{0:T(512)S(1)} %broadcast_multiply_fusion.8) | copy-start | bytes 4612
  285.3 25.3 %copy-start.48 = (f32[384]{0:T(512)}, f32[384]{0:T(512)S(1)}, u32[]{:S(2)}) copy-start(f32[384]{0:T(512)S(1)} %add_rsqrt_fusion.1) | copy-start | bytes 4612
  314.4 13.4 %all-to-all-start.5 = ((bf16[384,12,64]{0,2,1:T(8,128)(2,1)}), bf16[384,12,64]{0,2,1:T(8,128)(2,1)S(1)}, u32[]{:S(2)}, u32[]{:S(2)}) async-start(bf16[384,12,64]{0,2,1:T(8,128)(2,1)} %bitcast.50), calls=%async_computation.5 | async-start | bytes 1179648 | tf_op jit(solution)/shard_map/all_to_all | solution.py:270
  318.6 349.7 %reduce-scatter.26.cloned.1.call-start = ((), (), s32[]{:S(2)}) async-start(), calls=%async_computation.29 | async-start | bytes 884736
  478.9 196.7 %reduce-scatter.20.cloned.1.call-start = ((), (), s32[]{:S(2)}) async-start(), calls=%async_computation.26 | async-start | bytes 2433024 | tf_op jit(solution)/shard_map/reduce_scatter | solution.py:366
  482.5 237.1 %reduce-scatter.16.cloned.1.call-start = ((), (), s32[]{:S(2)}) async-start(), calls=%async_computation.24 | async-start | bytes 2433024 | tf_op jit(solution)/shard_map/reduce_scatter | solution.py:364
  507.7 316.3 %reduce-scatter.18.cloned.1.call-start = ((), (), s32[]{:S(2)}) async-start(), calls=%async_computation.25 | async-start | bytes 2433024 | tf_op jit(solution)/shard_map/reduce_scatter | solution.py:365
  526.5 402.1 %reduce-scatter.14.cloned.1.call-start = ((), (), s32[]{:S(2)}) async-start(), calls=%async_computation.23 | async-start | bytes 2433024 | tf_op jit(solution)/shard_map/reduce_scatter | solution.py:363
  557.9 512.2 %reduce-scatter.24.cloned.1.call-start = ((), (), s32[]{:S(2)}) async-start(), calls=%async_computation.28 | async-start | bytes 9732096 | tf_op jit(solution)/shard_map/reduce_scatter | solution.py:368
  567.6 644.1 %reduce-scatter.22.cloned.1.call-start = ((), (), s32[]{:S(2)}) async-start(), calls=%async_computation.27 | async-start | bytes 9732096 | tf_op jit(solution)/shard_map/reduce_scatter | solution.py:367
  592.1 77.8 %all-to-all-start.9 = ((bf16[8,2,18432]{2,1,0:T(2,128)(2,1)}), bf16[8,2,18432]{2,1,0:T(2,128)(2,1)S(1)}, u32[]{:S(2)}, u32[]{:S(2)}) async-start(bf16[8,2,18432]{2,1,0:T(2,128)(2,1)} %reshape.579), calls=%async_computation.9 | async-start | bytes 1179648 | tf_op jit(solution)/shard_map/all_to_all | solution.py:357
  595.6 27.9 %copy-start.52 = (f32[768]{0:T(1024)S(1)}, f32[768]{0:T(1024)}, u32[]{:S(2)}) copy-start(f32[768]{0:T(1024)} %get-tuple-element.617) | copy-start | bytes 9220
  595.7 27.9 %copy-start.53 = (f32[768]{0:T(1024)S(1)}, f32[768]{0:T(1024)}, u32[]{:S(2)}) copy-start(f32[768]{0:T(1024)} %get-tuple-element.708) | copy-start | bytes 9220
  595.7 27.9 %copy-start.54 = (f32[768]{0:T(1024)S(1)}, f32[768]{0:T(1024)}, u32[]{:S(2)}) copy-start(f32[768]{0:T(1024)} %get-tuple-element.706) | copy-start | bytes 9220
  595.7 27.9 %copy-start.57 = (f32[3072]{0:T(1024)S(1)}, f32[3072]{0:T(1024)}, u32[]{:S(2)}) copy-start(f32[3072]{0:T(1024)} %get-tuple-element.744) | copy-start | bytes 36868
  595.7 27.9 %copy-start.59 = (f32[768]{0:T(1024)S(1)}, f32[768]{0:T(1024)}, u32[]{:S(2)}) copy-start(f32[768]{0:T(1024)} %get-tuple-element.615) | copy-start | bytes 9220
  595.7 27.9 %copy-start.60 = (f32[768]{0:T(1024)S(1)}, f32[768]{0:T(1024)}, u32[]{:S(2)}) copy-start(f32[768]{0:T(1024)} %get-tuple-element.620) | copy-start | bytes 9220
  (75 other events, 366.9 us)
Sparse Core Ops, SparseCore 0:
  9.7 35.9 all-gather.14
  47.3 21.5 all-gather.12
  70.5 22.5 all-gather.10
  94.6 22.2 all-gather.16
  118.4 57.3 all-gather.18
  177.2 49.8 all-gather.20
  479.0 29.3 reduce-scatter.25
  514.3 100.1 reduce-scatter.19
  620.4 99.2 reduce-scatter.15
  725.4 98.6 reduce-scatter.17
  829.9 98.6 reduce-scatter.13
  934.9 135.1 reduce-scatter.23
  1076.6 135.0 reduce-scatter.21
where the time goes:
time: 1230 us; the launch traced here: 1220 us
  waiting for transfers between devices  555 us (45%)
  matrix products  223 us (18%)
  blocking collectives  212 us (17%)
  local copies, waits for them, and re-layouts  96.9 us (8%)
  other arithmetic  83.4 us (7%)
  starting transfers between devices  30.2 us (2%)
  between operations  17 us (1%)
    reduce_scatter x1, waiting for transfers between devices, shards(): lax.psum_scatter(w_in_grad, ('seq', 'fsdp'), scatter_dimension=0, tiled=T...  142 us
    reduce_scatter x1, waiting for transfers between devices, shards(): lax.psum_scatter(w_back_grad, ('seq', 'fsdp'), scatter_dimension=0, tiled...  142 us
    reduce_scatter x1, waiting for transfers between devices, shards(): lax.psum_scatter(w_query_grad, ('seq', 'fsdp'), scatter_dimension=0, tile...  105 us
    reduce_scatter x1, waiting for transfers between devices, shards(): lax.psum_scatter(w_value_grad, ('seq', 'fsdp'), scatter_dimension=0, tile...  104 us
    unnamed x3, blocking collectives  102 us
    reduce_scatter x1, waiting for transfers between devices, shards(): lax.psum_scatter(w_key_grad, ('seq', 'fsdp'), scatter_dimension=0, tiled=...  44.1 us
    unnamed x210, local copies, waits for them, and re-layouts  43.1 us
    dot_general x6, matrix products, scores_of(): jnp.einsum('ihd,jd->hij', block_pq, key_pos, preferred_element_type=jnp.f...  42.8 us
  transfers between devices with their start and end apart: 20, of which 8 were waited for; matrix products, arithmetic and copies ran while one was open for 19% of the time, Pallas kernels for 0%

commit v1 on v0

v1 whole, which is shorter than its diff:
```python
import jax
import jax.numpy as jnp
from jax import lax
from jax.experimental import pallas as pl
from jax.experimental.pallas import tpu as pltpu
from jax.sharding import PartitionSpec as P

DH = 64
LONGEST = 1024
QB = 256
BLOCKED = -1e30
BF = jnp.bfloat16
F32 = jnp.float32
VM = pl.BlockSpec(memory_space=pltpu.VMEM)
SM = pl.BlockSpec(memory_space=pltpu.SMEM)
VMEM_LIMIT = 60 * 1024 * 1024


def lanes_of(rows, width=128):
    return lax.broadcasted_iota(jnp.int32, (rows, width), 1)


def split3(value):
    high = value.astype(BF).astype(F32)
    rest = value - high
    middle = rest.astype(BF).astype(F32)
    return high, middle, rest - middle


def pick(lane, first, columns, base):
    for number, column in enumerate(columns):
        base = jnp.where(lane == first + number, column, base)
    return base


def project_body(place, x0, x1, x2, x3, w_ref, head_ref, tcol_ref, qx_ref, pq_ref, kx_ref, kxt_ref, vx_ref, vxt_ref, rolled):
    own, start, near = place[0], place[1], place[2]
    scale = DH ** -0.5
    rows = qx_ref.shape[1]
    part = x0.shape[0]
    for number, piece in enumerate((x0, x1, x2, x3)):
        y = jnp.dot(piece[...], w_ref[...], preferred_element_type=F32)
        base = pl.multiple_of((own ^ number) * part, 8)
        for c in range(5):
            column = y[:, c * 128 : (c + 1) * 128]
            rolled[c, pl.ds(base, part), :] = column
            rolled[c, pl.ds(pl.multiple_of(base + rows, 8), part), :] = column

    def block(r, carry):
        row = pl.multiple_of(r * QB, QB)
        lane = lanes_of(QB)
        kind = tcol_ref[pl.ds(row, QB), :]
        index = row + lax.broadcasted_iota(jnp.int32, (QB, 1), 0)
        small = index >= LONGEST
        first = jnp.where(small & (index < LONGEST + near), 1.0, 0.0)
        second = jnp.where(small & (index >= LONGEST + near), 1.0, 0.0)
        one = jnp.where(kind == 1, 1.0, 0.0)
        zero = 1.0 - one
        for h in range(3):
            both = rolled[h, pl.ds(start + row, QB), :].astype(BF).astype(F32)
            if h < 2:
                v = rolled[3, pl.ds(start + row, QB), :]
                v = v if h == 0 else pltpu.roll(v, 64, 1)
            else:
                v = rolled[4, pl.ds(start + row, QB), :]
            head = head_ref[h]
            content = (both + head[0:1]) * scale
            position = ((both + head[1:2]) * scale).astype(BF)
            typed = (both + head[2:3]) * scale
            differ = jnp.sum(typed * head[3:4], axis=1, keepdims=True)
            same = jnp.sum(typed * head[4:5], axis=1, keepdims=True)
            for_zero = jnp.where(kind == 1, differ, same)
            for_one = jnp.where(kind == 1, same, differ)
            columns = [*split3(for_zero), *split3(for_one), second * BLOCKED, first * BLOCKED]
            qx = pick(lane, 64, columns, jnp.where(lane < 64, content, 0.0)).astype(BF)
            qx_ref[h, pl.ds(row, QB), :] = qx
            raw = pltpu.roll(both, 64, 1)
            pq_ref[h, pl.ds(row, QB), :] = jnp.where(lane < 64, position.astype(F32), raw).astype(BF)
            kx = pick(lane, 64, [zero, zero, zero, one, one, one, first, second], jnp.where(lane < 64, raw, 0.0))
            kx_ref[h, pl.ds(row, QB), :] = kx.astype(BF)
            kxt_ref[h, :, pl.ds(row, QB)] = jnp.transpose(kx, (1, 0)).astype(BF)
            vx = jnp.where(lane < 64, v + head[5:6], jnp.where(lane < 67, 1.0, 0.0)).astype(BF)
            vx_ref[h, pl.ds(row, QB), :] = vx
            vxt_ref[h, :, pl.ds(row, QB)] = jnp.transpose(vx.astype(F32), (1, 0)).astype(BF)
        return carry

    lax.fori_loop(0, rows // QB, block, 0)


def project(place, pieces, w_qkv, head, tcol):
    rows = 4 * pieces[0].shape[0]
    tall = jax.ShapeDtypeStruct((3, rows, 128), BF)
    wide = jax.ShapeDtypeStruct((3, 128, rows), BF)
    return pl.pallas_call(
        project_body,
        in_specs=[SM] + [VM] * 7,
        out_specs=[VM] * 6,
        out_shape=[tall, tall, tall, wide, tall, wide],
        scratch_shapes=[pltpu.VMEM((5, 2 * rows, 128), F32)],
        compiler_params=pltpu.CompilerParams(vmem_limit_bytes=VMEM_LIMIT),
        cost_estimate=pl.CostEstimate(flops=2 * rows * 768 * 640, bytes_accessed=10_000_000, transcendentals=0),
        name="project",
    )(place, *pieces, w_qkv, head, tcol)


def attend_body(place, qx_ref, pq_ref, kxt_ref, vx_ref, kpt_ref, wrt_ref, sn_ref, cs_ref, big_ref, small_ref, ox_ref, o0, o1, o2, o3, keys, left, outs):
    h, i = pl.program_id(0), pl.program_id(1)
    own, start = place[0], place[1]
    width = kpt_ref.shape[0]
    half = width // 2
    rows = kpt_ref.shape[1]

    @pl.when((h == 0) & (i == 0))
    def _():
        keys[0:width, :] = kpt_ref[...]

    @pl.when(i == 0)
    def _():
        keys[width:, :] = kxt_ref[0]

    rel = jnp.dot(pq_ref[0], wrt_ref[0], preferred_element_type=F32)
    r1, r2 = rel[:, :half], rel[:, half:]
    sn, cs = sn_ref[...], cs_ref[...]
    left[:, 0:half] = (r1 * sn + r2 * cs).astype(BF)
    left[:, half:width] = (r2 * sn - r1 * cs).astype(BF)
    left[:, width:] = qx_ref[0]

    def attend(low, high, store):
        score = jnp.dot(left[...], keys[:, low:high], preferred_element_type=F32)
        top = jnp.max(score, axis=1, keepdims=True)
        raised = jnp.exp(score - top).astype(BF)
        store[0] = raised
        mixed = jnp.dot(raised, vx_ref[0, low:high, :], preferred_element_type=F32)
        inverse = 1.0 / mixed[:, 64:65]
        lane = lanes_of(QB)
        ox = jnp.where(lane < 64, mixed * inverse, jnp.where(lane == 64, inverse, 0.0))
        ox_ref[0] = ox
        row = pl.multiple_of(i * QB, QB)
        outs[h, pl.ds(row, QB), :] = ox
        outs[h, pl.ds(pl.multiple_of(row + rows, QB), QB), :] = ox

    @pl.when(i < LONGEST // QB)
    def _():
        attend(0, LONGEST, big_ref)

    @pl.when(i >= LONGEST // QB)
    def _():
        attend(LONGEST, rows, small_ref)

    @pl.when((h == 2) & (i == pl.num_programs(1) - 1))
    def _():
        part = o0.shape[0]
        for number, out in enumerate((o0, o1, o2, o3)):
            at = lax.rem((own ^ number) * part + rows - start, rows)
            out[...] = jnp.concatenate([outs[g, pl.ds(at, part), :][:, 0:64] for g in range(3)], axis=1).astype(BF)


def attend(place, qx, pq, kxt, vx, kpt, wrt, sn, cs):
    rows = qx.shape[1]
    width = kpt.shape[0]
    blocks = rows // QB
    bigs = LONGEST // QB
    rest = rows - LONGEST
    per_block = lambda h, i: (h, i, 0)
    per_head = lambda h, i: (h, 0, 0)
    whole2 = lambda h, i: (0, 0)
    part = rows // 4
    out_piece = jax.ShapeDtypeStruct((part, 192), BF)
    return pl.pallas_call(
        attend_body,
        grid=(3, blocks),
        in_specs=[
            SM,
            pl.BlockSpec((1, QB, 128), per_block),
            pl.BlockSpec((1, QB, 128), per_block),
            pl.BlockSpec((1, 128, rows), per_head),
            pl.BlockSpec((1, rows, 128), per_head),
            pl.BlockSpec((width, rows), whole2, pipeline_mode=pl.Buffered(1)),
            pl.BlockSpec((1, 128, width), per_head),
            pl.BlockSpec((QB, width // 2), lambda h, i: (i, 0)),
            pl.BlockSpec((QB, width // 2), lambda h, i: (i, 0)),
        ],
        out_specs=[
            pl.BlockSpec((1, QB, LONGEST), lambda h, i: (h, jnp.minimum(i, bigs - 1), 0)),
            pl.BlockSpec((1, QB, rest), lambda h, i: (h, jnp.maximum(i - bigs, 0), 0)),
            pl.BlockSpec((1, QB, 128), per_block),
        ]
        + [pl.BlockSpec((part, 192), whole2)] * 4,
        out_shape=[
            jax.ShapeDtypeStruct((3, LONGEST, LONGEST), BF),
            jax.ShapeDtypeStruct((3, rest, rest), BF),
            jax.ShapeDtypeStruct((3, rows, 128), F32),
        ]
        + [out_piece] * 4,
        scratch_shapes=[
            pltpu.VMEM((width + 128, rows), BF),
            pltpu.VMEM((QB, width + 128), BF),
            pltpu.VMEM((3, 2 * rows, 128), F32),
        ],
        compiler_params=pltpu.CompilerParams(vmem_limit_bytes=VMEM_LIMIT, dimension_semantics=("arbitrary", "arbitrary")),
        cost_estimate=pl.CostEstimate(flops=12_000_000_000, bytes_accessed=20_000_000, transcendentals=4_000_000),
        name="attend",
    )(place, qx, pq, kxt, vx, kpt, wrt, sn, cs)


def back_body(place, d0, d1, d2, d3, big_ref, small_ref, ox_ref, qx_ref, pq_ref, kx_ref, vxt_ref, kp_ref, wr_ref, sn_ref, cs_ref, tcol_ref, head_ref, g0, g1, g2, g3, gw_ref, sum_ref, keys, douts, dkt, dvt, grads):
    h, i = pl.program_id(0), pl.program_id(1)
    own, start = place[0], place[1]
    rows, width = kp_ref.shape
    half = width // 2
    scale = DH ** -0.5
    part = d0.shape[0]
    last = pl.num_programs(1) - 1
    row = pl.multiple_of(i * QB, QB)
    again = pl.multiple_of(row + rows, QB)

    @pl.when((h == 0) & (i == 0))
    def _():
        keys[:, 0:width] = kp_ref[...]
        blank = jnp.zeros((part, 64), F32)
        for number, piece in enumerate((d0, d1, d2, d3)):
            values = piece[...].astype(F32)
            base = pl.multiple_of((own ^ number) * part, 8)
            for g in range(3):
                padded = jnp.concatenate([values[:, g * 64 : (g + 1) * 64], blank], axis=1)
                douts[g, pl.ds(base, part), :] = padded
                douts[g, pl.ds(pl.multiple_of(base + rows, 8), part), :] = padded

    @pl.when(i == 0)
    def _():
        keys[:, width:] = kx_ref[0]
        dkt[...] = jnp.zeros_like(dkt)
        dvt[...] = jnp.zeros_like(dvt)
        gw_ref[...] = jnp.zeros_like(gw_ref)
        sum_ref[...] = jnp.zeros_like(sum_ref)

    lane = lanes_of(QB)
    dout = douts[h, pl.ds(start + row, QB), :]
    ox = ox_ref[0]
    inverse = ox[:, 64:65]
    dot_row = jnp.sum(dout * ox, axis=1, keepdims=True)
    dox = pick(lane, 64, [-x for x in split3(dot_row)], dout).astype(BF)
    dout_t = jnp.transpose(dout * inverse, (1, 0))[0:64].astype(BF)
    qx = qx_ref[0]
    qc_t = jnp.transpose(qx.astype(F32), (1, 0))[0:64].astype(BF)
    pq = pq_ref[0].astype(F32)
    qp_t = jnp.transpose(pq, (1, 0))[0:64].astype(BF)
    sn, cs = sn_ref[...], cs_ref[...]

    def back(low, high, saved):
        raised = saved[0]
        dprob = jnp.dot(dox, vxt_ref[0, :, low:high], preferred_element_type=F32)
        dscore = (raised.astype(F32) * (dprob * inverse)).astype(BF)
        dvt[:, low:high] += jnp.dot(dout_t, raised, preferred_element_type=F32)
        dkt[:, low:high] += jnp.dot(qc_t, dscore, preferred_element_type=F32)
        dleft = jnp.dot(dscore, keys[low:high, :], preferred_element_type=F32)
        da1, da2 = dleft[:, 0:half], dleft[:, half:width]
        drel = jnp.concatenate([(da1 * sn - da2 * cs).astype(BF), (da1 * cs + da2 * sn).astype(BF)], axis=1)
        dqp = jnp.dot(drel, wr_ref[0], preferred_element_type=F32)
        gw_ref[0] += jnp.dot(qp_t, drel, preferred_element_type=F32)
        dqx = dleft[:, width:]
        kind = tcol_ref[...]
        over_zero, over_one = dqx[:, 64:65], dqx[:, 67:68]
        same = jnp.where(kind == 1, over_one, over_zero)
        differ = jnp.where(kind == 1, over_zero, over_one)
        head = head_ref[0]
        dqt = differ * head[3:4] + same * head[4:5]
        dqc = jnp.where(lane < 64, dqx, 0.0)
        dq = (dqc + dqp + dqt) * scale
        grads[h, pl.ds(row, QB), :] = dq
        typed = (pltpu.roll(pq, 64, 1) + head[2:3]) * scale
        sums = [dqc * scale, dqp * scale, dqt * scale, differ * typed, same * typed]
        for number, values in enumerate(sums):
            sum_ref[0, number : number + 1, :] += jnp.sum(values, axis=0, keepdims=True)

    @pl.when(i < LONGEST // QB)
    def _():
        back(0, LONGEST, big_ref)

    @pl.when(i >= LONGEST // QB)
    def _():
        back(LONGEST, rows, small_ref)

    @pl.when(i == last)
    def _():
        dk = jnp.transpose(dkt[...], (1, 0))
        dq = grads[h, 0:rows, :]
        pair = jnp.concatenate([dq[:, 0:64], dk], axis=1)
        grads[h, 0:rows, :] = pair
        grads[h, rows : 2 * rows, :] = pair
        dv = jnp.transpose(dvt[...], (1, 0)).astype(BF).astype(F32)
        sum_ref[0, 5:6, 0:64] = jnp.sum(dv, axis=0, keepdims=True)
        blank = jnp.zeros_like(dv)

        @pl.when(h == 0)
        def _():
            padded = jnp.concatenate([dv, blank], axis=1)
            grads[3, 0:rows, :] = padded
            grads[3, rows : 2 * rows, :] = padded

        @pl.when(h == 1)
        def _():
            padded = grads[3, 0:rows, :] + jnp.concatenate([blank, dv], axis=1)
            grads[3, 0:rows, :] = padded
            grads[3, rows : 2 * rows, :] = padded

        @pl.when(h == 2)
        def _():
            padded = jnp.concatenate([dv, blank], axis=1)
            grads[4, 0:rows, :] = padded
            grads[4, rows : 2 * rows, :] = padded
            for number, out in enumerate((g0, g1, g2, g3)):
                at = lax.rem((own ^ number) * part + rows - start, rows)
                for c in range(5):
                    out[:, c * 128 : (c + 1) * 128] = grads[c, pl.ds(at, part), :].astype(BF)


def attend_back(place, douts, big, small, ox, qx, pq, kx, vxt, kp, wr, sn, cs, tcol, head):
    rows, width = kp.shape
    blocks = rows // QB
    bigs = LONGEST // QB
    rest = rows - LONGEST
    part = rows // 4
    per_block = lambda h, i: (h, i, 0)
    per_head = lambda h, i: (h, 0, 0)
    whole2 = lambda h, i: (0, 0)
    return pl.pallas_call(
        back_body,
        grid=(3, blocks),
        in_specs=[SM]
        + [pl.BlockSpec((part, 192), whole2)] * 4
        + [
            pl.BlockSpec((1, QB, LONGEST), lambda h, i: (h, jnp.minimum(i, bigs - 1), 0)),
            pl.BlockSpec((1, QB, rest), lambda h, i: (h, jnp.maximum(i - bigs, 0), 0)),
            pl.BlockSpec((1, QB, 128), per_block),
            pl.BlockSpec((1, QB, 128), per_block),
            pl.BlockSpec((1, QB, 128), per_block),
            pl.BlockSpec((1, rows, 128), per_head),
            pl.BlockSpec((1, 128, rows), per_head),
            pl.BlockSpec((rows, width), whole2, pipeline_mode=pl.Buffered(1)),
            pl.BlockSpec((1, width, 128), per_head),
            pl.BlockSpec((QB, width // 2), lambda h, i: (i, 0)),
            pl.BlockSpec((QB, width // 2), lambda h, i: (i, 0)),
            pl.BlockSpec((QB, 1), lambda h, i: (i, 0)),
            pl.BlockSpec((1, 8, 128), per_head),
        ],
        out_specs=[pl.BlockSpec((part, 640), whole2)] * 4
        + [pl.BlockSpec((1, 64, width), per_head), pl.BlockSpec((1, 8, 128), per_head)],
        out_shape=[jax.ShapeDtypeStruct((part, 640), BF)] * 4
        + [jax.ShapeDtypeStruct((3, 64, width), F32), jax.ShapeDtypeStruct((3, 8, 128), F32)],
        scratch_shapes=[
            pltpu.VMEM((rows, width + 128), BF),
            pltpu.VMEM((3, 2 * rows, 128), F32),
            pltpu.VMEM((64, rows), F32),
            pltpu.VMEM((64, rows), F32),
            pltpu.VMEM((5, 2 * rows, 128), F32),
        ],
        compiler_params=pltpu.CompilerParams(vmem_limit_bytes=VMEM_LIMIT, dimension_semantics=("arbitrary", "arbitrary")),
        cost_estimate=pl.CostEstimate(flops=20_000_000_000, bytes_accessed=25_000_000, transcendentals=0),
        name="attend_back",
    )(place, *douts, big, small, ox, qx, pq, kx, vxt, kp, wr, sn, cs, tcol, head)


EPS = 1e-09
HIGH = lax.Precision.HIGHEST


def norm_rows(values, gain_vec, shift_vec):
    center = values - jnp.mean(values, axis=-1, keepdims=True)
    inverse = lax.rsqrt(jnp.mean(center * center, axis=-1, keepdims=True) + EPS)
    normed = center * inverse
    return (normed * gain_vec + shift_vec, normed, inverse)


def norm_back(gradient, normed, inverse, gain_vec):
    scaled = gradient * gain_vec
    inner_term = scaled - jnp.mean(scaled, axis=-1, keepdims=True)
    inner_term = inner_term - normed * jnp.mean(scaled * normed, axis=-1, keepdims=True)
    return (inner_term * inverse, jnp.sum(gradient * normed, axis=0), jnp.sum(gradient, axis=0))


def angles_of(position, width):
    half_width = width // 2
    rate_table = 10000.0 ** (-(jnp.arange(half_width, dtype=jnp.float32) / half_width))
    turned = position.astype(jnp.float32)[:, None] * rate_table[None, :]
    return (jnp.sin(turned), jnp.cos(turned))


def contract_rows(left, right):
    return lax.dot_general(
        left, right, (((0,), (0,)), ((), ())), preferred_element_type=jnp.float32
    )


def contract_cols(left, right):
    return lax.dot_general(
        left, right, (((1,), (1,)), ((), ())), preferred_element_type=jnp.float32
    )


def across(values, other):
    seqs, fsdps = lax.axis_size("seq"), lax.axis_size("fsdp")
    pairs = []
    for s in range(seqs):
        for f in range(fsdps):
            to_s, to_f = other(s, f)
            pairs.append((s * fsdps + f, to_s * fsdps + to_f))
    return lax.ppermute(values, ("seq", "fsdp"), pairs)


def to_core(values):
    return across(values, lambda s, f: (s, f ^ 1))


def to_first(values):
    return across(values, lambda s, f: (s ^ (2 if f & 1 else 1), f))


def to_second(values):
    return across(values, lambda s, f: (s ^ (1 if f & 1 else 2), f))


def to_near(values):
    return across(values, lambda s, f: (s, f ^ 2))


def to_far(values):
    return across(values, lambda s, f: (s, f ^ 4))


def to_seq(values, k):
    return across(values, lambda s, f: (s ^ k, f))


def halve(kept, got, hops):
    kept, got = kept.astype(F32), [got.astype(F32)]
    count = kept.shape[0]
    for hop in hops:
        count //= 2
        out = kept[count : 2 * count]
        for g in got:
            out = out + g[count : 2 * count]
        got.append(hop(out.astype(BF)).astype(F32))
    total = kept[0]
    for g in got:
        total = total + g[0]
    return total


def back_blocks_body(place, u_ref, df_ref, keep_ref, send_ref):
    core = lax.rem(place[0], 2)
    group = u_ref.shape[1] // 4
    for g in range(1):
        acc = lax.dot_general(u_ref[...], df_ref[...], (((0,), (0,)), ((), ())), preferred_element_type=F32)
        at = pl.program_id(0) * 4
        for j in range(4):
            slot = place[1 + at + j]
            value = acc[j * group : (j + 1) * group].astype(BF)

            @pl.when(core == j % 2)
            def _():
                keep_ref[slot] = value

            @pl.when(core != j % 2)
            def _():
                send_ref[slot] = value


def back_blocks(place, u, df):
    rows, hidden = u.shape
    width = df.shape[1]
    out = jax.ShapeDtypeStruct((16, hidden // 32, width), BF)
    return pl.pallas_call(
        back_blocks_body,
        grid=(8,),
        in_specs=[SM, pl.BlockSpec((rows, hidden // 8), lambda g: (0, g)), pl.BlockSpec((rows, width), lambda g: (0, 0))],
        out_specs=[pl.BlockSpec((16, hidden // 32, width), lambda g: (0, 0, 0))] * 2,
        out_shape=[out, out],
        compiler_params=pltpu.CompilerParams(vmem_limit_bytes=VMEM_LIMIT, dimension_semantics=("arbitrary",)),
        cost_estimate=pl.CostEstimate(flops=2 * rows * hidden * width, bytes_accessed=8_000_000, transcendentals=0),
        name="back_blocks",
    )(place, u, df)


def in_blocks_body(place, h_ref, dz_ref, a_ref, db_ref, vec_ref, keep_ref, send_ref):
    core = lax.rem(place[0], 2)
    own = lax.div(place[0], 8)
    step = pl.program_id(0)

    def put(block, odd, low, value):
        slot = place[1 + block]
        high = low + value.shape[0]

        @pl.when(core == odd)
        def _():
            keep_ref[slot, low:high, :] = value

        @pl.when(core != odd)
        def _():
            send_ref[slot, low:high, :] = value

    def chunk(which):
        for g in range(2):
            acc = lax.dot_general(
                h_ref[:, g * 384 : (g + 1) * 384], dz_ref[...], (((0,), (0,)), ((), ())), preferred_element_type=F32
            )
            for j in range(16):
                put(g * 16 + j, j % 2, which * 24, acc[j * 24 : (j + 1) * 24].astype(BF))

    for which in range(4):
        pl.when(step == which)(lambda which=which: chunk(which))

    @pl.when(step == 4)
    def _():
        for g in range(2):
            acc = lax.dot_general(
                a_ref[:, g * 384 : (g + 1) * 384], db_ref[...], (((0,), (0,)), ((), ())), preferred_element_type=F32
            )
            for j in range(16):
                block = (own ^ (2 * g + j // 8)) * 8 + j % 8
                put(block, j % 2, 96, acc[j * 24 : (j + 1) * 24].astype(BF))
        for j in range(32):
            put(j, j % 2, 120, vec_ref[j])


def in_blocks(place, hidden_low, dz, attn, dbr, vec):
    rows, width = hidden_low.shape
    chunks = dz.shape[1] // width
    out = jax.ShapeDtypeStruct((16, 128, width), BF)
    whole = pl.BlockSpec((rows, width), lambda g: (0, 0))
    return pl.pallas_call(
        in_blocks_body,
        grid=(chunks + 1,),
        in_specs=[
            SM,
            whole,
            pl.BlockSpec((rows, width), lambda g: (0, jnp.minimum(g, chunks - 1))),
            whole,
            whole,
            pl.BlockSpec((32, 8, width), lambda g: (0, 0, 0)),
        ],
        out_specs=[pl.BlockSpec((16, 128, width), lambda g: (0, 0, 0))] * 2,
        out_shape=[out, out],
        compiler_params=pltpu.CompilerParams(vmem_limit_bytes=VMEM_LIMIT, dimension_semantics=("arbitrary",)),
        cost_estimate=pl.CostEstimate(flops=2 * rows * width * (dz.shape[1] + width), bytes_accessed=12_000_000, transcendentals=0),
        name="in_blocks",
    )(place, hidden_low, dz, attn, dbr, vec)


def shards(
    inputs,
    w_query,
    w_key,
    w_value,
    b_value,
    w_out,
    b_out,
    norm1_gain,
    norm1_bias,
    w_in,
    b_in,
    w_back,
    b_back,
    norm2_gain,
    norm2_bias,
    w_relative,
    bias_content,
    bias_position,
    bias_type,
    type_embed,
    lengths,
    token_types,
    owners,
    grad_output,
):
    seqs, fsdps = lax.axis_size("seq"), lax.axis_size("fsdp")
    direct = seqs == 4 and fsdps == 8
    own, rank = lax.axis_index("seq"), lax.axis_index("fsdp")
    pack_count = owners.shape[0]
    sliver_rows = inputs.shape[1]
    width = inputs.shape[2]
    local_rows = w_query.shape[0]
    local_cols = width // seqs
    local_heads = w_relative.shape[1]
    scale = DH ** -0.5
    owner_table = owners[None, :] == jnp.arange(pack_count, dtype=jnp.int32)[:, None]
    owner_low = owner_table.astype(BF)
    dealt = jnp.dot(
        owner_low, inputs.reshape(pack_count, sliver_rows * width), preferred_element_type=F32
    )
    dealt = dealt.astype(BF).reshape(pack_count, sliver_rows, width)
    mine = lax.all_to_all(dealt, "fsdp", split_axis=0, concat_axis=1, tiled=True)[0]
    row_count = mine.shape[0]
    chosen = (owners == rank).astype(jnp.int32)
    pack_types = jnp.sum(chosen[:, None] * token_types, axis=0)
    pack_sizes = jnp.sum(chosen[:, None] * lengths, axis=0)
    pack_rows = pack_types.shape[0]

    def head_columns(weight):
        return lax.dynamic_slice_in_dim(weight, own * local_cols, local_cols, 1)

    paired = jnp.concatenate(
        [
            head_columns(w_query).reshape(local_rows, local_heads, DH),
            head_columns(w_key).reshape(local_rows, local_heads, DH),
        ],
        axis=2,
    ).reshape(local_rows, 2 * local_cols)
    block = jnp.concatenate(
        [paired, head_columns(w_value), w_relative.reshape(local_rows, local_cols)], axis=1
    )
    long_vectors = (b_value, b_out, norm1_gain, norm1_bias, b_back, norm2_gain, norm2_bias, b_in)
    head_vectors = (bias_content, bias_position, bias_type, type_embed)
    vector = jnp.concatenate([v.reshape(-1) for v in long_vectors + head_vectors])
    extra = -(-vector.shape[0] // width)
    extra = -(-extra // 8) * 8
    vector = jnp.pad(vector, (0, extra * width - vector.shape[0])).reshape(extra, width)
    early = lax.all_gather(jnp.concatenate([block, vector], axis=0), "fsdp", axis=0)
    qkvr = early[:, :local_rows].reshape(width, width)
    vectors = early[:, local_rows:].reshape(fsdps, extra * width).astype(F32)
    at, full = 0, []
    for v in long_vectors:
        full.append(vectors[:, at : at + v.shape[0]].reshape(-1))
        at += v.shape[0]
    bv_full, bo_full, gain_one, shift_one, bback_full, gain_two, shift_two, bin_full = full
    heads = []
    for v in head_vectors:
        each = vectors[:, at : at + v.size].reshape((fsdps,) + v.shape)
        heads.append(jnp.moveaxis(each, 0, -2).reshape(v.shape[:-1] + (DH,)))
        at += v.size
    content_full, position_full, typebias_full, embed_full = heads
    bv_own = lax.dynamic_slice_in_dim(bv_full, own * local_cols, local_cols, 0)
    head = jnp.stack(
        [
            content_full,
            position_full,
            typebias_full,
            embed_full[0],
            embed_full[1],
            bv_own.reshape(local_heads, DH),
        ],
        axis=1,
    )
    head = jnp.pad(head, ((0, 0), (0, 2), (0, 64)))

    def quarter(weight):
        rows = weight.shape[0] // seqs
        return lax.dynamic_slice_in_dim(weight, own * rows, rows, 0)

    def gather_all(weight):
        return lax.all_gather(quarter(weight), ("fsdp", "seq"), axis=0, tiled=True)

    wo_full = gather_all(w_out)
    win_full = gather_all(w_in)
    wback_full = gather_all(w_back)
    order = own ^ jnp.arange(seqs, dtype=jnp.int32)
    wo_near = jnp.take(wo_full.reshape(seqs, local_cols, width), order, axis=0).reshape(width, width)

    longest = jnp.argmax(pack_sizes).astype(jnp.int32)
    start = jnp.sum(jnp.where(jnp.arange(3) < longest, pack_sizes, 0))
    near = jnp.sum(jnp.where(jnp.arange(3) == (longest + 1) % 3, pack_sizes, 0))
    place = jnp.stack([own, start, near]).astype(jnp.int32)
    row_index = jnp.arange(pack_rows, dtype=jnp.int32)
    position = jnp.where(
        row_index < LONGEST,
        row_index,
        jnp.where(row_index < LONGEST + near, row_index - LONGEST, row_index - LONGEST - near),
    )
    sine, cosine = angles_of(position, width)
    key_pos = jnp.concatenate([cosine, sine], axis=-1).astype(BF)
    key_pos_t = key_pos.T
    turned_types = lax.dynamic_slice_in_dim(
        jnp.concatenate([pack_types, pack_types]), start, pack_rows, 0
    )[:, None]
    wrel = qkvr[:, 3 * local_cols :].reshape(width, local_heads, DH)
    wrel_rows = jnp.pad(jnp.transpose(wrel, (1, 0, 2)), ((0, 0), (0, 0), (0, 64)))
    wrel_cols = jnp.pad(jnp.transpose(wrel, (1, 2, 0)), ((0, 0), (0, 64), (0, 0)))
    w_qkv = qkvr[:, :640]

    pieces = [mine] + [to_seq(mine, k) for k in range(1, 4)]
    qx, pq, kx, kxt, vx, vxt = project(place, pieces, w_qkv, head, turned_types)
    big, small, ox, *head_out = attend(place, qx, pq, kxt, vx, key_pos_t, wrel_cols, sine, cosine)
    attn_rows = jnp.concatenate(
        [head_out[0]] + [to_seq(head_out[k], k) for k in range(1, 4)], axis=1
    )
    branch = jnp.dot(attn_rows, wo_near, preferred_element_type=F32) + bo_full
    first_sum = mine.astype(F32) + branch
    hidden_one, normed_one, inverse_one = norm_rows(first_sum, gain_one, shift_one)
    hidden_low = hidden_one.astype(BF)
    pre_act = jnp.dot(hidden_low, win_full, preferred_element_type=F32) + bin_full
    act_low = jax.nn.gelu(pre_act).astype(BF)
    ffn_out = jnp.dot(act_low, wback_full, preferred_element_type=F32) + bback_full
    second_sum = hidden_one + ffn_out
    result, normed_two, inverse_two = norm_rows(second_sum, gain_two, shift_two)
    activations = result.astype(BF).reshape(1, row_count, width)
    out_grad = grad_output[0].astype(F32)
    sum_two_grad, gain_two_grad, shift_two_grad = norm_back(
        out_grad, normed_two, inverse_two, gain_two
    )
    ffn_grad = sum_two_grad.astype(BF)
    back_bias_grad = jnp.sum(ffn_grad.astype(F32), axis=0)
    act_grad = contract_cols(ffn_grad, wback_full)
    pre_grad = jax.vjp(jax.nn.gelu, pre_act)[1](act_grad)[0].astype(BF)
    in_bias_grad = jnp.sum(pre_grad.astype(F32), axis=0)
    hidden_grad = sum_two_grad + contract_cols(pre_grad, win_full)
    sum_one_grad, gain_one_grad, shift_one_grad = norm_back(
        hidden_grad, normed_one, inverse_one, gain_one
    )
    branch_grad = sum_one_grad.astype(BF)
    out_bias_grad = jnp.sum(branch_grad.astype(F32), axis=0)
    attn_grad = contract_cols(branch_grad, wo_near).astype(BF)
    douts = [attn_grad[:, k * local_cols : (k + 1) * local_cols] for k in range(4)]
    douts = [douts[0]] + [to_seq(douts[k], k) for k in range(1, 4)]
    short = (gain_one_grad, shift_one_grad, gain_two_grad, shift_two_grad, out_bias_grad, back_bias_grad)
    devices = seqs * fsdps
    if direct:
        relative = jnp.arange(32, dtype=jnp.int32) ^ (own * 8 + rank)
        bit = lambda n: (relative >> n) & 1
        flip = (bit(0) ^ (rank & 1)) == 1
        slots = jnp.where(flip, bit(4), bit(3)) * 8 + jnp.where(flip, bit(3), bit(4)) * 4 + bit(1) * 2 + bit(2)
        table = jnp.concatenate([(own * 8 + rank)[None], slots]).astype(jnp.int32)
        hops = (to_first, to_second, to_near, to_far)
        kept, sent = back_blocks(table, act_low, ffn_grad)
        back_total = halve(kept, to_core(sent), hops)
        vec = jnp.concatenate(
            [v.reshape(32, -1) for v in short] + [in_bias_grad.reshape(32, -1)], axis=1
        )
        vec = jnp.pad(vec.astype(BF)[:, None, :], ((0, 0), (0, 7), (0, width - vec.shape[1])))
        kept, sent = in_blocks(table, hidden_low, pre_grad, attn_rows, branch_grad, vec)
        in_total = halve(kept, to_core(sent), hops)
        w_back_grad = back_total
        w_in_grad = jnp.concatenate([in_total[c * 24 : (c + 1) * 24] for c in range(4)], axis=1)
        w_out_grad = in_total[96:120]
        row = in_total[120]
        short_grads = [row[n * 24 : (n + 1) * 24] for n in range(6)]
        in_bias_grad = row[144:240]
    else:
        scatter = lambda v: lax.psum_scatter(v, ("seq", "fsdp"), scatter_dimension=0, tiled=True)
        w_back_grad = scatter(contract_rows(act_low, ffn_grad))
        w_in_grad = scatter(contract_rows(hidden_low, pre_grad))
        turned = contract_rows(attn_rows, branch_grad).reshape(seqs, local_cols, width)
        w_out_grad = scatter(jnp.take(turned, order, axis=0).reshape(width, width))
        short_grads = [scatter(v) for v in short]
        in_bias_grad = scatter(in_bias_grad)

    *turned, rel_grad, sums = attend_back(
        place, douts, big, small, ox, qx, pq, kx, vxt, key_pos, wrel_rows, sine, cosine, turned_types, head
    )
    dx = [contract_cols(t, w_qkv) for t in turned]
    input_rows = sum_one_grad + dx[0]
    for k in range(1, 4):
        input_rows = input_rows + to_seq(dx[k].astype(BF), k).astype(F32)
    input_rows = input_rows.astype(BF)
    returned = lax.all_to_all(
        input_rows.reshape(1, row_count, width), "fsdp", split_axis=1, concat_axis=0, tiled=True
    )
    input_grad = contract_rows(owner_low, returned.reshape(pack_count, sliver_rows * width))
    input_grad = input_grad.astype(BF).reshape(pack_count, sliver_rows, width)

    qkv_grad = contract_rows(jnp.concatenate(pieces, axis=0), jnp.concatenate(turned, axis=0))
    fine = width // devices
    qkv_grad = qkv_grad[:, : 3 * local_cols].reshape(seqs, fsdps, fine, 3 * local_cols)
    qkv_grad = jnp.transpose(qkv_grad, (1, 0, 2, 3)).reshape(fsdps, local_rows, 3 * local_cols)
    rel_grad = jnp.transpose(rel_grad, (2, 0, 1)).reshape(fsdps, local_rows, local_cols)
    sums = sums[:, :, :DH]
    eighth = DH // fsdps
    spread = lambda v, n: jnp.moveaxis(v.reshape(v.shape[:-1] + (fsdps, n)), -2, 0).reshape(fsdps, -1)
    vec = jnp.concatenate(
        [
            sums[:, 5].reshape(fsdps, fine),
            spread(sums[:, 0], eighth),
            spread(sums[:, 1], eighth),
            spread(sums[:, 2], eighth),
            spread(jnp.stack([sums[:, 3], sums[:, 4]]), eighth),
        ],
        axis=1,
    )
    vec = jnp.pad(vec[:, None, :], ((0, 0), (0, 7), (0, width - vec.shape[1])))
    bundle = jnp.concatenate([jnp.concatenate([qkv_grad, rel_grad], axis=2), vec], axis=1)
    if direct:
        count = jnp.arange(8, dtype=jnp.int32)
        wanted = rank ^ (((count >> 2) & 1) | (((count >> 1) & 1) << 1) | ((count & 1) << 2))
        bundle = jnp.take(bundle.astype(BF), wanted, axis=0)
        total = halve(bundle[:4], to_core(bundle[4:]), (to_near, to_far))
    else:
        total = lax.psum_scatter(bundle, "fsdp", scatter_dimension=0, tiled=True)[0]
    own_qkv = total[:local_rows, : 3 * local_cols].reshape(seqs, fine, 3 * local_cols).astype(BF)
    swapped = lax.all_to_all(own_qkv, "seq", split_axis=0, concat_axis=0, tiled=True).astype(F32)
    both = swapped[:, :, : 2 * local_cols].reshape(seqs, fine, local_heads, 2, DH)
    both = jnp.transpose(both, (3, 1, 0, 2, 4)).reshape(2, fine, width)
    w_value_grad = jnp.transpose(swapped[:, :, 2 * local_cols :], (1, 0, 2)).reshape(fine, width)
    rel_total = total[:local_rows, 3 * local_cols :].reshape(local_rows, local_heads, DH)
    row = total[local_rows]
    cut = local_heads * eighth
    value_bias_grad = row[:fine]
    bias_grads = [row[fine + n * cut : fine + (n + 1) * cut].reshape(local_heads, eighth) for n in range(3)]
    embed_grad = row[fine + 3 * cut : fine + 5 * cut].reshape(2, local_heads, eighth)
    return (
        activations,
        input_grad,
        both[0],
        both[1],
        w_value_grad,
        value_bias_grad,
        w_out_grad,
        short_grads[4],
        short_grads[0],
        short_grads[1],
        w_in_grad,
        in_bias_grad,
        w_back_grad,
        short_grads[5],
        short_grads[2],
        short_grads[3],
        rel_total,
        bias_grads[0],
        bias_grads[1],
        bias_grads[2],
        embed_grad,
    )


def solution(mesh):
    placed = (
        P(None, ("seq", "fsdp"), None),
        P("fsdp", None),
        P("fsdp", None),
        P("fsdp", None),
        P("fsdp"),
        P("fsdp", None),
        P("fsdp"),
        P("fsdp"),
        P("fsdp"),
        P("fsdp", None),
        P("fsdp"),
        P("fsdp", None),
        P("fsdp"),
        P("fsdp"),
        P("fsdp"),
        P("fsdp", "seq", None),
        P("seq", "fsdp"),
        P("seq", "fsdp"),
        P("seq", "fsdp"),
        P(None, "seq", "fsdp"),
        P(),
        P(),
        P(),
        P("fsdp", "seq", None),
    )
    return jax.shard_map(
        shards,
        mesh=mesh,
        in_specs=placed,
        out_specs=(
            P("fsdp", "seq", None),
            P(None, ("seq", "fsdp"), None),
            P(("seq", "fsdp"), None),
            P(("seq", "fsdp"), None),
            P(("seq", "fsdp"), None),
            P(("seq", "fsdp")),
            P(("seq", "fsdp"), None),
            P(("seq", "fsdp")),
            P(("seq", "fsdp")),
            P(("seq", "fsdp")),
            P(("seq", "fsdp"), None),
            P(("seq", "fsdp")),
            P(("seq", "fsdp"), None),
            P(("seq", "fsdp")),
            P(("seq", "fsdp")),
            P(("seq", "fsdp")),
            P("fsdp", "seq", None),
            P("seq", "fsdp"),
            P("seq", "fsdp"),
            P("seq", "fsdp"),
            P(None, "seq", "fsdp"),
        ),
        check_vma=False,
    )
```

time: 1230 us -> 497 us (0.40)
  waiting for transfers between devices: 555 us -> 151 us
  blocking collectives: 212 us -> 0 us
  matrix products: 223 us -> 31.1 us
  Pallas kernels: 0 us -> 102 us
  local copies, waits for them, and re-layouts: 96.9 us -> 67.8 us
    reduce_scatter x6 -> x0, waiting for transfers between devices: 536 us -> none  [the longest x1 142 us: shards(): lax.psum_scatter(w_in_grad, ('seq', 'fsdp'), scatter_dimension=0, tiled=T...]
    dot_general x42 -> x3, matrix products: 183 us -> 14.3 us  [the longest x1 8.23 us: shards(): jnp.dot(hidden_low, win_full, preferred_element_type=F32) + bin_full]
    unnamed x3 -> x0, blocking collectives: 102 us -> none
    pallas_call x0 -> x5, Pallas kernels: none -> 102 us  [the longest x1 36.3 us: attend_back(): pl.pallas_call(back_body, grid=(3, blocks), in_specs=[SM] + [pl.BlockSpec...]
    all_gather x6 -> x4, waiting for transfers between devices: 0.06 us -> 86.2 us  [the longest x3 86.2 us: gather_all(): return lax.all_gather(quarter(weight), ('fsdp', 'seq'), axis=0, tiled=True)]
    all_gather x6 -> x0, blocking collectives: 76 us -> none  [the longest x1 20.3 us: shards(): lax.all_gather(w_relative, 'fsdp', axis=0, tiled=True)]
    ppermute x0 -> x25, waiting for transfers between devices: none -> 49.3 us  [across(): return lax.ppermute(values, ('seq', 'fsdp'), pairs)]
    all_to_all x3 -> x0, blocking collectives: 33.4 us -> none  [the longest x1 12.5 us: shards(): lax.all_to_all(key_grad.astype(jnp.bfloat16), 'seq', split_axis=0, concat...]
  transfers between devices with their start and end apart: 20 -> 32, of which waited for: 8 -> 13; matrix products, arithmetic and copies ran while one was open for 19% -> 28% of each run, Pallas kernels for 0% -> 21%
where the time goes in v1:
time: 497 us; the launch traced here: 488 us
  waiting for transfers between devices  151 us (30%)
  Pallas kernels  102 us (21%)
  other arithmetic  78.8 us (16%)
  local copies, waits for them, and re-layouts  67.8 us (14%)
  starting transfers between devices  38.5 us (8%)
  matrix products  31.1 us (6%)
  between operations  18.5 us (4%)
    all_gather x3, waiting for transfers between devices, gather_all(): return lax.all_gather(quarter(weight), ('fsdp', 'seq'), axis=0, tiled=True)  86.2 us
    ppermute x25, waiting for transfers between devices, across(): return lax.ppermute(values, ('seq', 'fsdp'), pairs)  49.3 us
    pallas_call x1, Pallas kernels, attend_back(): pl.pallas_call(back_body, grid=(3, blocks), in_specs=[SM] + [pl.BlockSpec...  36.3 us
    pallas_call x1, Pallas kernels, attend(): pl.pallas_call(attend_body, grid=(3, blocks), in_specs=[SM, pl.BlockSpec(...  30.2 us
    ppermute x25, starting transfers between devices, across(): return lax.ppermute(values, ('seq', 'fsdp'), pairs)  24.9 us
    convert_element_type x17, other arithmetic, halve(): got.append(hop(out.astype(BF)).astype(F32))  21.3 us
    convert_element_type x6, other arithmetic, halve(): kept, got = (kept.astype(F32), [got.astype(F32)])  17 us
    all_to_all x1, waiting for transfers between devices, shards(): lax.all_to_all(own_qkv, 'seq', split_axis=0, concat_axis=0, tiled=True)  14.1 us
  transfers between devices with their start and end apart: 32, of which 13 were waited for; matrix products, arithmetic and copies ran while one was open for 28% of the time, Pallas kernels for 21%

profile of v1, /device:TPU:0, one launch (start us, length us, event | category | flops | bytes accessed | tf_op | source)
XLA Modules:
  0.0 488.0 jit_solution(11951520336829042972)
XLA Ops:
  10.4 5.4 %concatenate.75 = bf16[1176]{0:T(1024)(128)(2,1)S(1)} concatenate(bf16[96]{0:T(256)(128)(2,1)} %param.28, bf16[96]{0:T(256)(128)(2,1)} %param.30, bf16[96]{0:T(256)(128)(2,1)} %param.31, bf16[96]{0:T(256)(128)(2,1)} %param.32, bf16[96]{0:T(256)(128)(2,1)} %param.36, bf16[96]{0:T(256)(128)(2,1)} %param.37, bf16[96]{0:T(256)(128)(2,1)} %param.38, bf16[384]{0:T(512)(128)(2,1)} %param.34, ...), dimensions={0} | concatenate | bytes 4704 | tf_op jit(solution)/shard_map/concatenate | solution.py:614
  22.3 1.6 constant_dynamic-slice_fusion
  25.4 6.4 %all-to-all-start = ((bf16[8,48,768]{2,1,0:T(8,128)(2,1)}), bf16[8,48,768]{2,1,0:T(8,128)(2,1)S(1)}, u32[]{:S(2)}, u32[]{:S(2)}) async-start(bf16[8,48,768]{2,1,0:T(8,128)(2,1)} %copy.166), calls=%async_computation | async-start | bytes 1179648 | tf_op jit(solution)/shard_map/all_to_all | solution.py:592
  37.8 10.1 %multiply_cosine_fusion = (f32[1536,384]{1,0:T(8,128)}, bf16[1536,384]{1,0:T(8,128)(2,1)S(1)}, bf16[1536,384]{1,0:T(8,128)(2,1)S(1)}, f32[1536,384]{1,0:T(8,128)}) fusion(f32[384]{0:T(512)S(1)} %negate_power_fusion, f32[1536]{0:T(1024)S(1)} %fusion.58), kind=kLoop, calls=%fused_computation.16 | loop fusion | flops 1769472 | bytes 7085568 | tf_op jit(solution)/shard_map/cos | solution.py:386
  48.0 1.8 pad_maximum_fusion
  51.0 2.5 copy.179.kpt_ref
  55.5 1.9 pad_add_fusion.place
  70.6 4.6 collective-permute-done.x1
  75.2 12.7 %collective-permute-done.1.x2 = bf16[384,768]{1,0:T(8,128)(2,1)} collective-permute-done((bf16[384,768]{1,0:T(8,128)(2,1)S(1)}, bf16[384,768]{1,0:T(8,128)(2,1)}, u32[]{:S(2)}, u32[]{:S(2)}) %collective-permute-start.1) | collective-permute-done | bytes 589856 | tf_op jit(solution)/shard_map/ppermute | solution.py:408
  89.4 14.0 %project.1 = (bf16[3,1536,128]{2,1,0:T(8,128)(2,1)}, bf16[3,1536,128]{2,1,0:T(8,128)(2,1)}, bf16[3,1536,128]{2,1,0:T(8,128)(2,1)}, bf16[3,128,1536]{2,1,0:T(8,12...) custom-call(s32[3]{0:T(128)} %pad_add_fusion.place, bf16[384,768]{1,0:T(8,128)(2,1)} %bitcast.156, ...), custom_call_target="tpu_custom_call" | custom-call | flops 1509949440 | bytes 10000000 | tf_op jit(solution)/shard_map/project/pallas_call | solution.py:94
  103.4 30.2 %attend.1 = (bf16[3,1024,1024]{2,1,0:T(8,128)(2,1)}, bf16[3,512,512]{2,1,0:T(8,128)(2,1)}, f32[3,1536,128]{2,1,0:T(8,128)}, bf16[384,192]{1,0:T(8,128)(2,1)}, bf...) custom-call(s32[3]{0:T(128)} %pad_add_fusion.place, ...), custom_call_target="tpu_custom_call" | custom-call | flops 12000000000 | bytes 20000000 | tf_op jit(solution)/shard_map/attend/pallas_call | solution.py:169
  141.1 2.0 gather_fusion
  144.1 3.3 collective-permute-done.4
  150.7 29.8 %all-gather.8.cloned.1.call-done = bf16[768,3072]{1,0:T(8,128)(2,1)} async-done(((bf16[24,3072]{1,0:T(8,128)(2,1)}), bf16[768,3072]{1,0:T(8,128)(2,1)}) %all-gather.8.cloned.1.call-update) | async-done | bytes 4718608 | tf_op jit(solution)/shard_map/all_gather | solution.py:651
  180.5 8.2 %multiply_convert_fusion = (bf16[384,3072]{1,0:T(8,128)(2,1)}, f32[384,3072]{1,0:T(8,128)}) fusion(f32[3072]{0:T(1024)} %add.323, bf16[384,768]{1,0:T(8,128)(2,1)S(1)} %fusion.42.h_ref, bf16[768,3072]{1,0:T(8,128)(2,1)} %all-gather.8.cloned.1.call-done), kind=kOutput, calls=%fused_computation.13 | convolution fusion | flops 1823735808 | bytes 12398592 | tf_op jit(solution)/shard_map/dot_general | solution.py:690
  188.7 56.4 %all-gather.10.cloned.1.call-done = bf16[3072,768]{1,0:T(8,128)(2,1)} async-done(((bf16[96,768]{1,0:T(8,128)(2,1)}), bf16[3072,768]{1,0:T(8,128)(2,1)}) %all-gather.10.cloned.1.call-update) | async-done | bytes 4718608 | tf_op jit(solution)/shard_map/all_gather | solution.py:651
  245.1 5.4 %fusion.101 = (f32[384]{0:T(512)S(1)}, f32[384,768]{1,0:T(8,128)S(1)}) fusion(f32[768]{0:T(1024)} %add.329, bf16[384,3072]{1,0:T(8,128)(2,1)} %get-tuple-element.240.u_ref, bf16[3072,768]{1,0:T(8,128)(2,1)} %all-gather.10.cloned.1.call-done, f32[768]{0:T(1024)} %add.320, f32[768]{0:T(1024)} %mul.211, f32[384]{0:T(512)} %copy-done.28, ...), kind=kOutput, calls=%fused_computation.246 | convolution fusion | flops 1814003328 | bytes 9451008 | tf_op jit(solution)/shard_map/dot_general | solution.py:692
  250.8 1.9 fusion.40
  253.8 5.7 %fusion.90 = (bf16[3072]{0:T(1024)(128)(2,1)}, bf16[384,3072]{1,0:T(8,128)(2,1)S(1)}) fusion(f32[384,3072]{1,0:T(8,128)S(1)} %copy-done.51, bf16[384,768]{1,0:T(8,128)(2,1)S(1)} %get-tuple-element.195.df_ref, bf16[3072,768]{1,0:T(8,128)(2,1)S(1)} %copy-done.43), kind=kOutput, calls=%fused_computation.237 | convolution fusion | flops 1836708864 | bytes 12392448 | tf_op jit(solution)/shard_map/dot_general | solution.py:396
  259.6 3.1 multiply_reduce_fusion
  262.7 2.0 fusion.94
  271.7 12.3 %in_blocks.1 = (bf16[16,128,768]{2,1,0:T(8,128)(2,1)}, bf16[16,128,768]{2,1,0:T(8,128)(2,1)}) custom-call(s32[33]{0:T(128)} %pad_add_fusion.1.place, bf16[384,768]{1,0:T(8,128)(2,1)} %copy-done.14, bf16[384,3072]{1,0:T(8,128)(2,1)} %copy-done.50, bf16[384,768]{1,0:T(8,128)(2,1)} %copy-done.18, bf16[384,768]{1,0:T(8,128)(2,1)} %copy-done.13, ...), custom_call_target="tpu_custom_call" | custom-call | flops 2264924160 | bytes 12000000 | tf_op jit(solution)/shard_map/in_blocks/pallas_call | solution.py:531
  284.0 5.2 %convert_element_type.220 = f32[16,128,768]{2,1,0:T(8,128)} convert(bf16[16,128,768]{2,1,0:T(8,128)(2,1)} %get-tuple-element.65) | non-fusion elementwise | flops 1572864 | bytes 9437184 | tf_op jit(solution)/shard_map/convert_element_type | solution.py:436
  289.1 9.3 %back_blocks.1 = (bf16[16,96,768]{2,1,0:T(8,128)(2,1)}, bf16[16,96,768]{2,1,0:T(8,128)(2,1)}) custom-call(s32[33]{0:T(128)} %pad_add_fusion.1.place, bf16[384,3072]{1,0:T(8,128)(2,1)} %get-tuple-element.240.u_ref, bf16[384,768]{1,0:T(8,128)(2,1)} %copy-done.19), custom_call_target="tpu_custom_call" | custom-call | flops 1811939328 | bytes 8000000 | tf_op jit(solution)/shard_map/back_blocks/pallas_call | solution.py:473
  298.9 4.3 convert_element_type.229
  304.1 36.3 %attend_back.1 = (bf16[384,640]{1,0:T(8,128)(2,1)}, bf16[384,640]{1,0:T(8,128)(2,1)}, bf16[384,640]{1,0:T(8,128)(2,1)}, bf16[384,640]{1,0:T(8,128)(2,1)}, f32[3,64,768]{2,1,0:T(8,128)}, /*index=5*/f32[3,8,128]{2,1,0:T(8,128)}) custom-call(s32[3]{0:T(128)} %pad_add_fusion.place, bf16[384,192]{1,0:T(8,128)(2,1)} %get-tuple-element.207.d0, ...), custom_call_target="tpu_custom_call" | custom-call | flops 20000000000 | bytes 25000000 | tf_op jit(solution)/shard_map/attend_back/pallas_call | solution.py:327
  344.0 3.9 fusion.10
  348.9 1.7 copy.183
  351.0 1.9 gather_fusion.1
  362.6 2.3 convert_element_type.230
  365.0 5.0 %convert_element_type.221 = f32[16,128,768]{2,1,0:T(8,128)S(1)} convert(bf16[16,128,768]{2,1,0:T(8,128)(2,1)} %collective-permute-done.15) | non-fusion elementwise | flops 1572864 | bytes 9437184 | tf_op jit(solution)/shard_map/convert_element_type | solution.py:436
  370.2 1.8 fusion.7
  377.8 7.2 %collective-permute-done.10 = bf16[384,768]{1,0:T(8,128)(2,1)S(1)} collective-permute-done((bf16[384,768]{1,0:T(8,128)(2,1)S(1)}, bf16[384,768]{1,0:T(8,128)(2,1)S(1)}, u32[]{:S(2)}, u32[]{:S(2)}) %collective-permute-start.10) | collective-permute-done | bytes 589856 | tf_op jit(solution)/shard_map/ppermute | solution.py:408
  387.1 4.2 reduce.57
  394.3 3.3 all-to-all-start.2
  401.6 14.1 %all-to-all-done.2 = bf16[4,24,576]{2,1,0:T(8,128)(2,1)S(1)} async-done(((bf16[4,24,576]{2,1,0:T(8,128)(2,1)}), bf16[4,24,576]{2,1,0:T(8,128)(2,1)S(1)}, u32[]{:S(2)}, u32[]{:S(2)}) %all-to-all-start.2) | async-done | bytes 110624 | tf_op jit(solution)/shard_map/all_to_all | solution.py:788
  415.7 3.8 all-to-all-start.1
  421.2 2.6 fusion.41
  425.1 1.7 convert_element_type.223
  426.8 4.2 fusion.25
  436.1 1.8 reshape.573
  438.0 4.7 bitcast_reduce_fusion
  447.5 1.6 fusion.43
  449.1 1.7 collective-permute-start.18
  452.0 3.6 collective-permute-done.23
  458.2 7.6 %collective-permute-done.18 = bf16[2,128,768]{2,1,0:T(8,128)(2,1)S(1)} collective-permute-done((bf16[2,128,768]{2,1,0:T(8,128)(2,1)S(1)}, bf16[2,128,768]{2,1,0:T(8,128)(2,1)S(1)}, u32[]{:S(2)}, u32[]{:S(2)}) %collective-permute-start.18) | collective-permute-done | bytes 393248 | tf_op jit(solution)/shard_map/ppermute | solution.py:408
  467.4 1.9 fusion.56
  469.3 8.0 %collective-permute-done.19 = bf16[1,128,768]{2,1,0:T(8,128)(2,1)S(1)} collective-permute-done((bf16[1,128,768]{2,1,0:T(8,128)(2,1)S(1)}, bf16[1,128,768]{2,1,0:T(8,128)(2,1)S(1)}, u32[]{:S(2)}, u32[]{:S(2)}) %collective-permute-start.19) | collective-permute-done | bytes 196640 | tf_op jit(solution)/shard_map/ppermute | solution.py:408
  (356 shorter events, 104.3 us)
Async XLA Ops:
  7.2 14.3 %copy-start = (bf16[96,3072]{1,0:T(8,128)(2,1)S(1)}, bf16[96,3072]{1,0:T(8,128)(2,1)}, u32[]{:S(2)}) copy-start(bf16[96,3072]{1,0:T(8,128)(2,1)} %param.33) | copy-start | bytes 1769476
  7.2 54.9 %all-gather.12.cloned.1.call-start = ((), (), s32[]{:S(2)}) async-start(), calls=%async_computation.6 | async-start | bytes 1437696 | tf_op jit(solution)/shard_map/all_gather | solution.py:618
  15.8 8.1 %copy-start.15 = (bf16[8,48,768]{2,1,0:T(8,128)(2,1)S(1)}, bf16[8,48,768]{2,1,0:T(8,128)(2,1)}, u32[]{:S(2)}) copy-start(bf16[8,48,768]{2,1,0:T(8,128)(2,1)} %param.24) | copy-start | bytes 1769476
  20.0 121.1 %all-gather.6.cloned.1.call-start = ((), (), s32[]{:S(2)}) async-start(), calls=%async_computation.3 | async-start | bytes 1216512 | tf_op jit(solution)/shard_map/all_gather | solution.py:651
  21.5 159.0 %all-gather.8.cloned.1.call-start = ((), (), s32[]{:S(2)}) async-start(), calls=%async_computation.4 | async-start | bytes 4866048 | tf_op jit(solution)/shard_map/all_gather | solution.py:651
  22.2 222.9 %all-gather.10.cloned.1.call-start = ((), (), s32[]{:S(2)}) async-start(), calls=%async_computation.5 | async-start | bytes 4866048 | tf_op jit(solution)/shard_map/all_gather | solution.py:651
  24.4 7.3 %copy-start.41 = (s32[8,3]{0,1:T(4,128)S(1)}, s32[8,3]{0,1:T(4,128)}, u32[]{:S(2)}) copy-start(s32[8,3]{0,1:T(4,128)} %param.44) | copy-start | bytes 292
  24.4 13.3 %copy-start.22 = (s32[8,1536]{1,0:T(8,128)S(1)}, s32[8,1536]{1,0:T(8,128)}, u32[]{:S(2)}) copy-start(s32[8,1536]{1,0:T(8,128)} %param.45) | copy-start | bytes 147460
  25.4 33.2 %all-to-all-start = ((bf16[8,48,768]{2,1,0:T(8,128)(2,1)}), bf16[8,48,768]{2,1,0:T(8,128)(2,1)S(1)}, u32[]{:S(2)}, u32[]{:S(2)}) async-start(bf16[8,48,768]{2,1,0:T(8,128)(2,1)} %copy.166), calls=%async_computation | async-start | bytes 1179648 | tf_op jit(solution)/shard_map/all_to_all | solution.py:592
  58.6 16.6 %collective-permute-start = (bf16[384,768]{1,0:T(8,128)(2,1)S(1)}, bf16[384,768]{1,0:T(8,128)(2,1)}, u32[]{:S(2)}, u32[]{:S(2)}) collective-permute-start(bf16[384,768]{1,0:T(8,128)(2,1)S(1)} %bitcast.153), channel_id=1, source_target_pairs={{0,8},{1,9},{2,10},{3,11},{4,12},{5,13},{6,14},{7,15},{8,0},{9,1},... | collective-permute-start | bytes 1769480 | tf_op jit(solution)/shard_map/ppermute | solution.py:408
  60.1 27.8 %collective-permute-start.1 = (bf16[384,768]{1,0:T(8,128)(2,1)S(1)}, bf16[384,768]{1,0:T(8,128)(2,1)}, u32[]{:S(2)}, u32[]{:S(2)}) collective-permute-start(bf16[384,768]{1,0:T(8,128)(2,1)S(1)} %bitcast.154), channel_id=1, source_target_pairs={{0,16},{1,17},{2,18},{3,19},{4,20},{5,21},{6,22},{7,23},{8,24},{9,... | collective-permute-start | bytes 1769480 | tf_op jit(solution)/shard_map/ppermute | solution.py:408
  61.4 28.0 %collective-permute-start.2 = (bf16[384,768]{1,0:T(8,128)(2,1)S(1)}, bf16[384,768]{1,0:T(8,128)(2,1)}, u32[]{:S(2)}, u32[]{:S(2)}) collective-permute-start(bf16[384,768]{1,0:T(8,128)(2,1)S(1)} %bitcast.155), channel_id=1, source_target_pairs={{0,24},{1,25},{2,26},{3,27},{4,28},{5,29},{6,30},{7,31},{8,16},{9,... | collective-permute-start | bytes 1769480 | tf_op jit(solution)/shard_map/ppermute | solution.py:408
  133.6 10.5 %collective-permute-start.5 = (bf16[384,192]{1,0:T(8,128)(2,1)}, bf16[384,192]{1,0:T(8,128)(2,1)S(1)}, u32[]{:S(2)}, u32[]{:S(2)}) collective-permute-start(bf16[384,192]{1,0:T(8,128)(2,1)} %get-tuple-element.53), channel_id=1, source_target_pairs={{0,24},{1,25},{2,26},{3,27},{4,28},{5,29},{6,30},{7,31},{8,16},{9,... | collective-permute-start | bytes 442376 | tf_op jit(solution)/shard_map/ppermute | solution.py:408
  135.1 12.3 %collective-permute-start.4 = (bf16[384,192]{1,0:T(8,128)(2,1)}, bf16[384,192]{1,0:T(8,128)(2,1)S(1)}, u32[]{:S(2)}, u32[]{:S(2)}) collective-permute-start(bf16[384,192]{1,0:T(8,128)(2,1)} %get-tuple-element.52), channel_id=1, source_target_pairs={{0,16},{1,17},{2,18},{3,19},{4,20},{5,21},{6,22},{7,23},{8,24},{9,... | collective-permute-start | bytes 442376 | tf_op jit(solution)/shard_map/ppermute | solution.py:408
  136.4 11.7 %collective-permute-start.3 = (bf16[384,192]{1,0:T(8,128)(2,1)}, bf16[384,192]{1,0:T(8,128)(2,1)S(1)}, u32[]{:S(2)}, u32[]{:S(2)}) collective-permute-start(bf16[384,192]{1,0:T(8,128)(2,1)} %get-tuple-element.51), channel_id=1, source_target_pairs={{0,8},{1,9},{2,10},{3,11},{4,12},{5,13},{6,14},{7,15},{8,0},{9,1},... | collective-permute-start | bytes 442376 | tf_op jit(solution)/shard_map/ppermute | solution.py:408
  150.7 38.0 %copy-start.14 = (bf16[384,768]{1,0:T(8,128)(2,1)}, bf16[384,768]{1,0:T(8,128)(2,1)S(1)}, u32[]{:S(2)}) copy-start(bf16[384,768]{1,0:T(8,128)(2,1)S(1)} %fusion.42.h_ref) | copy-start | bytes 1769476
  245.1 8.6 %copy-start.51 = (f32[384,3072]{1,0:T(8,128)S(1)}, f32[384,3072]{1,0:T(8,128)}, u32[]{:S(2)}) copy-start(f32[384,3072]{1,0:T(8,128)} %get-tuple-element.241) | copy-start | bytes 14155780
  252.8 6.8 %slice-start.4 = ((s8[4718592]{0:T(1024)(128)(4,1)}), s8[4194304]{0:T(1024)(128)(4,1)S(1)}, s32[]{:S(2)}) async-start(s8[4718592]{0:T(1024)(128)(4,1)} %bitcast.176), calls=%async_computation.11 | async-start | bytes 8388608
  253.8 5.8 %copy-start.27 = (f32[384]{0:T(512)S(1)}, f32[384]{0:T(512)}, u32[]{:S(2)}) copy-start(f32[384]{0:T(512)} %copy-done.26) | copy-start | bytes 4612
  266.4 36.9 %collective-permute-start.6 = (bf16[384,192]{1,0:T(8,128)(2,1)S(1)}, bf16[384,192]{1,0:T(8,128)(2,1)S(1)}, u32[]{:S(2)}, u32[]{:S(2)}) collective-permute-start(bf16[384,192]{1,0:T(8,128)(2,1)S(1)} %get-tuple-element.206), channel_id=1, source_target_pairs={{0,8},{1,9},{2,10},{3,11},{4,12},{5,13},{6,14},{7,15},{8,0},{9,1},... | collective-permute-start | bytes 442376 | tf_op jit(solution)/shard_map/ppermute | solution.py:408
  267.8 35.5 %collective-permute-start.7 = (bf16[384,192]{1,0:T(8,128)(2,1)S(1)}, bf16[384,192]{1,0:T(8,128)(2,1)S(1)}, u32[]{:S(2)}, u32[]{:S(2)}) collective-permute-start(bf16[384,192]{1,0:T(8,128)(2,1)S(1)} %get-tuple-element.205), channel_id=1, source_target_pairs={{0,16},{1,17},{2,18},{3,19},{4,20},{5,21},{6,22},{7,23},{8,24},{9,... | collective-permute-start | bytes 442376 | tf_op jit(solution)/shard_map/ppermute | solution.py:408
  268.4 34.9 %collective-permute-start.8 = (bf16[384,192]{1,0:T(8,128)(2,1)S(1)}, bf16[384,192]{1,0:T(8,128)(2,1)S(1)}, u32[]{:S(2)}, u32[]{:S(2)}) collective-permute-start(bf16[384,192]{1,0:T(8,128)(2,1)S(1)} %get-tuple-element.204), channel_id=1, source_target_pairs={{0,24},{1,25},{2,26},{3,27},{4,28},{5,29},{6,30},{7,31},{8,16},{9,... | collective-permute-start | bytes 442376 | tf_op jit(solution)/shard_map/ppermute | solution.py:408
  284.0 81.0 %collective-permute-start.15 = (bf16[16,128,768]{2,1,0:T(8,128)(2,1)}, bf16[16,128,768]{2,1,0:T(8,128)(2,1)}, u32[]{:S(2)}, u32[]{:S(2)}) collective-permute-start(bf16[16,128,768]{2,1,0:T(8,128)(2,1)} %get-tuple-element.66), channel_id=1, source_target_pairs={{0,1},{1,0},{2,3},{3,2},{4,5},{5,4},{6,7},{7,6},{8,9},{9,8},{10,11... | collective-permute-start | bytes 9437192 | tf_op jit(solution)/shard_map/ppermute | solution.py:408
  298.4 62.9 %collective-permute-start.20 = (bf16[16,96,768]{2,1,0:T(8,128)(2,1)}, bf16[16,96,768]{2,1,0:T(8,128)(2,1)}, u32[]{:S(2)}, u32[]{:S(2)}) collective-permute-start(bf16[16,96,768]{2,1,0:T(8,128)(2,1)} %get-tuple-element.68), channel_id=1, source_target_pairs={{0,1},{1,0},{2,3},{3,2},{4,5},{5,4},{6,7},{7,6},{8,9},{9,8},{10,11... | collective-permute-start | bytes 7077896 | tf_op jit(solution)/shard_map/ppermute | solution.py:408
  354.5 5.9 %collective-permute-start.12 = (bf16[4,104,768]{2,1,0:T(8,128)(2,1)S(1)}, bf16[4,104,768]{2,1,0:T(8,128)(2,1)S(1)}, u32[]{:S(2)}, u32[]{:S(2)}) collective-permute-start(bf16[4,104,768]{2,1,0:T(8,128)(2,1)S(1)} %get-tuple-element.202), channel_id=1, source_target_pairs={{0,1},{1,0},{2,3},{3,2},{4,5},{5,4},{6,7},{7,6},{8,9},{9,8},{10,11... | collective-permute-start | bytes 1916936 | tf_op jit(solution)/shard_map/ppermute | solution.py:408
  356.1 20.8 %collective-permute-start.11 = (bf16[384,768]{1,0:T(8,128)(2,1)S(1)}, bf16[384,768]{1,0:T(8,128)(2,1)S(1)}, u32[]{:S(2)}, u32[]{:S(2)}) collective-permute-start(bf16[384,768]{1,0:T(8,128)(2,1)S(1)} %convolution_convert_fusion.2), channel_id=1, source_target_pairs={{0,24},{1,25},{2,26},{3,27},{4,28},{5,29},{6,30},{7,31},{8,16},{9,... | collective-permute-start | bytes 1769480 | tf_op jit(solution)/shard_map/ppermute | solution.py:408
  358.3 26.7 %collective-permute-start.10 = (bf16[384,768]{1,0:T(8,128)(2,1)S(1)}, bf16[384,768]{1,0:T(8,128)(2,1)S(1)}, u32[]{:S(2)}, u32[]{:S(2)}) collective-permute-start(bf16[384,768]{1,0:T(8,128)(2,1)S(1)} %convolution_convert_fusion.3), channel_id=1, source_target_pairs={{0,16},{1,17},{2,18},{3,19},{4,20},{5,21},{6,22},{7,23},{8,24},{9,... | collective-permute-start | bytes 1769480 | tf_op jit(solution)/shard_map/ppermute | solution.py:408
  360.4 24.5 %collective-permute-start.9 = (bf16[384,768]{1,0:T(8,128)(2,1)S(1)}, bf16[384,768]{1,0:T(8,128)(2,1)S(1)}, u32[]{:S(2)}, u32[]{:S(2)}) collective-permute-start(bf16[384,768]{1,0:T(8,128)(2,1)S(1)} %convolution_convert_fusion.4), channel_id=1, source_target_pairs={{0,8},{1,9},{2,10},{3,11},{4,12},{5,13},{6,14},{7,15},{8,0},{9,1},... | collective-permute-start | bytes 1769480 | tf_op jit(solution)/shard_map/ppermute | solution.py:408
  361.2 15.6 %copy-start.7 = (f32[4,104,768]{2,1,0:T(8,128)}, f32[4,104,768]{2,1,0:T(8,128)S(1)}, u32[]{:S(2)}) copy-start(f32[4,104,768]{2,1,0:T(8,128)S(1)} %convert_element_type.210) | copy-start | bytes 3833860
  361.3 14.8 %collective-permute-start.13 = (bf16[2,104,768]{2,1,0:T(8,128)(2,1)S(1)}, bf16[2,104,768]{2,1,0:T(8,128)(2,1)S(1)}, u32[]{:S(2)}, u32[]{:S(2)}) collective-permute-start(bf16[2,104,768]{2,1,0:T(8,128)(2,1)S(1)} %fusion.46), channel_id=1, source_target_pairs={{0,2},{1,3},{2,0},{3,1},{4,6},{5,7},{6,4},{7,5},{8,10},{9,11},{10,... | collective-permute-start | bytes 958472 | tf_op jit(solution)/shard_map/ppermute | solution.py:408
  362.6 7.4 %slice-start = ((s8[6291456]{0:T(1024)(128)(4,1)}), s8[4194304]{0:T(1024)(128)(4,1)S(1)}, s32[]{:S(2)}) async-start(s8[6291456]{0:T(1024)(128)(4,1)} %bitcast.127), calls=%async_computation.7 | async-start | bytes 8388608
  362.6 12.2 %slice-start.2 = ((s8[4718592]{0:T(1024)(128)(4,1)}), s8[4194304]{0:T(1024)(128)(4,1)S(1)}, s32[]{:S(2)}) async-start(s8[4718592]{0:T(1024)(128)(4,1)} %bitcast.129), calls=%async_computation.9 | async-start | bytes 8388608
  364.9 9.9 %copy-start.3 = (f32[16,96,768]{2,1,0:T(8,128)}, f32[16,96,768]{2,1,0:T(8,128)S(1)}, u32[]{:S(2)}) copy-start(f32[16,96,768]{2,1,0:T(8,128)S(1)} %convert_element_type.230) | copy-start | bytes 14155780
  365.0 9.9 %slice-start.3 = ((s8[4718592]{0:T(1024)(128)(4,1)}), s8[524288]{0:T(1024)(128)(4,1)S(1)}, s32[]{:S(2)}) async-start(s8[4718592]{0:T(1024)(128)(4,1)} %bitcast.129), calls=%async_computation.10 | async-start | bytes 1048576
  373.4 51.7 %collective-permute-start.16 = (bf16[8,128,768]{2,1,0:T(8,128)(2,1)}, bf16[8,128,768]{2,1,0:T(8,128)(2,1)}, u32[]{:S(2)}, u32[]{:S(2)}) collective-permute-start(bf16[8,128,768]{2,1,0:T(8,128)(2,1)} %fusion.7), channel_id=1, source_target_pairs={{0,8},{1,17},{2,10},{3,19},{4,12},{5,21},{6,14},{7,23},{8,0},{9,25... | collective-permute-start | bytes 4718600 | tf_op jit(solution)/shard_map/ppermute | solution.py:408
  376.1 8.8 %copy-start.8 = (f32[384,768]{1,0:T(8,128)S(1)}, f32[384,768]{1,0:T(8,128)}, u32[]{:S(2)}) copy-start(f32[384,768]{1,0:T(8,128)} %get-tuple-element.198) | copy-start | bytes 3538948
  376.1 8.8 %copy-start.20 = (bf16[384,640]{1,0:T(8,128)(2,1)S(1)}, bf16[384,640]{1,0:T(8,128)(2,1)}, u32[]{:S(2)}) copy-start(bf16[384,640]{1,0:T(8,128)(2,1)} %get-tuple-element.59) | copy-start | bytes 1474564
  376.1 43.6 %collective-permute-start.21 = (bf16[8,96,768]{2,1,0:T(8,128)(2,1)}, bf16[8,96,768]{2,1,0:T(8,128)(2,1)}, u32[]{:S(2)}, u32[]{:S(2)}) collective-permute-start(bf16[8,96,768]{2,1,0:T(8,128)(2,1)} %fusion.9), channel_id=1, source_target_pairs={{0,8},{1,17},{2,10},{3,19},{4,12},{5,21},{6,14},{7,23},{8,0},{9,25... | collective-permute-start | bytes 3538952 | tf_op jit(solution)/shard_map/ppermute | solution.py:408
  376.8 8.9 %copy-start.9 = (f32[2,104,768]{2,1,0:T(8,128)}, f32[2,104,768]{2,1,0:T(8,128)S(1)}, u32[]{:S(2)}) copy-start(f32[2,104,768]{2,1,0:T(8,128)S(1)} %convert_element_type.212) | copy-start | bytes 1916932
  376.9 15.5 %collective-permute-start.14 = (bf16[1,104,768]{2,1,0:T(8,128)(2,1)S(1)}, bf16[1,104,768]{2,1,0:T(8,128)(2,1)S(1)}, u32[]{:S(2)}, u32[]{:S(2)}) collective-permute-start(bf16[1,104,768]{2,1,0:T(8,128)(2,1)S(1)} %fusion.51), channel_id=1, source_target_pairs={{0,4},{1,5},{2,6},{3,7},{4,0},{5,1},{6,2},{7,3},{8,12},{9,13},{10,... | collective-permute-start | bytes 479240 | tf_op jit(solution)/shard_map/ppermute | solution.py:408
  394.3 21.4 %all-to-all-start.2 = ((bf16[4,24,576]{2,1,0:T(8,128)(2,1)}), bf16[4,24,576]{2,1,0:T(8,128)(2,1)S(1)}, u32[]{:S(2)}, u32[]{:S(2)}) async-start(bf16[4,24,576]{2,1,0:T(8,128)(2,1)} %bitcast.37), calls=%async_computation.2 | async-start | bytes 245760 | tf_op jit(solution)/shard_map/all_to_all | solution.py:788
  415.7 20.4 %all-to-all-start.1 = ((bf16[8,2,18432]{2,1,0:T(2,128)(2,1)}), bf16[8,2,18432]{2,1,0:T(2,128)(2,1)S(1)}, u32[]{:S(2)}, u32[]{:S(2)}) async-start(bf16[8,2,18432]{2,1,0:T(2,128)(2,1)} %reshape.572), calls=%async_computation.1 | async-start | bytes 1179648 | tf_op jit(solution)/shard_map/all_to_all | solution.py:754
  423.9 19.1 %collective-permute-start.22 = (bf16[4,96,768]{2,1,0:T(8,128)(2,1)}, bf16[4,96,768]{2,1,0:T(8,128)(2,1)}, u32[]{:S(2)}, u32[]{:S(2)}) collective-permute-start(bf16[4,96,768]{2,1,0:T(8,128)(2,1)} %fusion.41), channel_id=1, source_target_pairs={{0,16},{1,9},{2,18},{3,11},{4,20},{5,13},{6,22},{7,15},{8,24},{9,1... | collective-permute-start | bytes 1769480 | tf_op jit(solution)/shard_map/ppermute | solution.py:408
  431.0 15.2 %collective-permute-start.17 = (bf16[4,128,768]{2,1,0:T(8,128)(2,1)}, bf16[4,128,768]{2,1,0:T(8,128)(2,1)}, u32[]{:S(2)}, u32[]{:S(2)}) collective-permute-start(bf16[4,128,768]{2,1,0:T(8,128)(2,1)} %fusion.25), channel_id=1, source_target_pairs={{0,16},{1,9},{2,18},{3,11},{4,20},{5,13},{6,22},{7,15},{8,24},{9,1... | collective-permute-start | bytes 2359304 | tf_op jit(solution)/shard_map/ppermute | solution.py:408
  445.7 9.9 %collective-permute-start.23 = (bf16[2,96,768]{2,1,0:T(8,128)(2,1)S(1)}, bf16[2,96,768]{2,1,0:T(8,128)(2,1)S(1)}, u32[]{:S(2)}, u32[]{:S(2)}) collective-permute-start(bf16[2,96,768]{2,1,0:T(8,128)(2,1)S(1)} %fusion.48), channel_id=1, source_target_pairs={{0,2},{1,3},{2,0},{3,1},{4,6},{5,7},{6,4},{7,5},{8,10},{9,11},{10,... | collective-permute-start | bytes 884744 | tf_op jit(solution)/shard_map/ppermute | solution.py:408
  449.1 16.7 %collective-permute-start.18 = (bf16[2,128,768]{2,1,0:T(8,128)(2,1)S(1)}, bf16[2,128,768]{2,1,0:T(8,128)(2,1)S(1)}, u32[]{:S(2)}, u32[]{:S(2)}) collective-permute-start(bf16[2,128,768]{2,1,0:T(8,128)(2,1)S(1)} %fusion.43), channel_id=1, source_target_pairs={{0,2},{1,3},{2,0},{3,1},{4,6},{5,7},{6,4},{7,5},{8,10},{9,11},{10,... | collective-permute-start | bytes 1179656 | tf_op jit(solution)/shard_map/ppermute | solution.py:408
  456.8 10.5 %collective-permute-start.24 = (bf16[1,96,768]{2,1,0:T(8,128)(2,1)S(1)}, bf16[1,96,768]{2,1,0:T(8,128)(2,1)S(1)}, u32[]{:S(2)}, u32[]{:S(2)}) collective-permute-start(bf16[1,96,768]{2,1,0:T(8,128)(2,1)S(1)} %fusion.54), channel_id=1, source_target_pairs={{0,4},{1,5},{2,6},{3,7},{4,0},{5,1},{6,2},{7,3},{8,12},{9,13},{10,... | collective-permute-start | bytes 442376 | tf_op jit(solution)/shard_map/ppermute | solution.py:408
  467.1 10.2 %collective-permute-start.19 = (bf16[1,128,768]{2,1,0:T(8,128)(2,1)S(1)}, bf16[1,128,768]{2,1,0:T(8,128)(2,1)S(1)}, u32[]{:S(2)}, u32[]{:S(2)}) collective-permute-start(bf16[1,128,768]{2,1,0:T(8,128)(2,1)S(1)} %fusion.49), channel_id=1, source_target_pairs={{0,4},{1,5},{2,6},{3,7},{4,0},{5,1},{6,2},{7,3},{8,12},{9,13},{10,... | collective-permute-start | bytes 589832 | tf_op jit(solution)/shard_map/ppermute | solution.py:408
  (42 other events, 145.5 us)
Sparse Core Ops, SparseCore 0:
  20.1 35.7 all-gather.11
  59.4 53.8 all-gather.5
  116.2 64.1 all-gather.7
  183.2 61.8 all-gather.9
